TPU v7x, 128 devices: a whole 4x4x4 slice. The times are simulated.
128 devices in a mesh: own: 128 (over z, x, y, core).
Axes of the slice: x: 4, y: 4, z: 4, core: 2. Of those that a mesh axis runs over, the one named last changes fastest.
Arguments:
- sentence_vectors: bfloat16 [65536, 1024], P('own'), may hold values from -12 to 12
- group_assignment: int32 [65536, 1], P('own'), may hold values from 0 to 511; in each aligned block of 512 rows (0 to 511, 512 to 1023, ...) at most 2 rows name the same one
- adjacent_importance: bfloat16 [65536], P('own'), may hold values from 0.099609375 to 10
- group_sharpness: bfloat16 [512], P('own'), may hold values from 8 to 32
Outputs:
- smoothed: bfloat16 [65536, 1024], P('own')
- dup_score: bfloat16 [65536], P('own')
Inputs may be any that keep to these rules, and one draw needn't show every extreme that they name: `group_assignment`: of the rows of one device, at most 2 name the same cluster; every cluster is named by some row.
All inputs are finite; a program needn't handle non-finite values.
Results may differ from a plain program's by a relative error of at most 0.0056.
Values may be sent and summed in bfloat16 or wider, within the bound.
No kernel may reach another device: no remote copies, remote signals or barrier semaphores. Data moves between devices by JAX's collectives and lax.ppermute only.
A program may use at most 64 MiB of HBM per device.

v0:
```python
import jax
import jax.numpy as jnp
from jax import lax
from jax.sharding import PartitionSpec as P


def pick_block(whole, wanted):
    block_size = min(whole, wanted)
    while whole % block_size != 0:
        block_size = block_size // 2
    return block_size


def block_ranks(ident):
    count = ident.shape[0]
    positions = jnp.arange(count, dtype=jnp.int32)
    same = (ident[:, None] == ident[None, :]) & (positions[None, :] < positions[:, None])
    return jnp.sum(same.astype(jnp.int32), axis=1)


def unit_of(rows):
    widened = rows.astype(jnp.float32)
    square_sum = jnp.sum(widened * widened, axis=1)
    return (widened * lax.rsqrt(square_sum + 1e-06)[:, None]).astype(jnp.bfloat16)


def place_rows(onehot, values):
    return lax.dot_general(
        onehot, values, (((0,), (0,)), ((), ())), preferred_element_type=jnp.float32
    ).astype(jnp.bfloat16)


def compact(weight):
    slot_count = weight.shape[0]
    live = (weight > 0).astype(jnp.int32)
    positions = jnp.arange(slot_count, dtype=jnp.int32)
    earlier = (positions[None, :] < positions[:, None]).astype(jnp.int32)
    live_before = jnp.sum(earlier * live[None, :], axis=1)
    dead_before = positions - live_before
    live_count = jnp.sum(live)
    target = jnp.where(live > 0, live_before, live_count + dead_before)
    perm = (target[:, None] == positions[None, :]).astype(jnp.bfloat16)
    return (perm, live_count)


def key_sweep(q_unit, q_pos, unit_rows, key_rows, key_weight, exponent_sharpness, live_count):
    slot_count = unit_rows.shape[0]
    key_block = pick_block(slot_count, 256)
    totals = jnp.zeros((q_unit.shape[0],), jnp.float32)
    numer = jnp.zeros((q_unit.shape[0], key_rows.shape[1]), jnp.float32)
    key_start = 0

    def add_block(carry, key_start=key_start):
        cosine = lax.dot_general(
            q_unit, unit_rows, (((1,), (1,)), ((), ())), preferred_element_type=jnp.float32
        )
        columns = key_start + jnp.arange(key_block, dtype=jnp.int32)
        cosine = jnp.where(q_pos[:, None] == columns[None, :], jnp.float32(0.0), cosine)
        weights = key_weight.astype(jnp.float32)
        expo = weights[None, :] * jnp.exp(exponent_sharpness * (cosine - 1.0))
        tot_now = jnp.sum(expo, axis=1)
        num_now = jnp.dot(expo.astype(jnp.bfloat16), key_rows, preferred_element_type=jnp.float32)
        return (tot_now, num_now)

    def keep_block(carry):
        return carry

    totals, numer = lax.cond(key_start < live_count, add_block, keep_block, (totals, numer))
    return (totals, numer)


def finish(totals, numer, exponent_sharpness):
    positive = totals > 0
    safe = jnp.where(positive, totals, jnp.float32(1.0))
    smooth = jnp.where(positive[:, None], numer / safe[:, None], jnp.float32(0.0)).astype(
        jnp.bfloat16
    )
    score = jnp.where(positive, jnp.log(safe) + exponent_sharpness, jnp.float32(0.0)).astype(
        jnp.bfloat16
    )
    return (smooth, score)


def cluster_share(rows, weight, exponent_sharpness, half, parts):
    perm, live_count = compact(weight)
    packed = place_rows(perm, rows)
    packed_weight = place_rows(perm, weight[:, None])[:, 0]
    unit_rows = unit_of(packed)
    slot_count = rows.shape[0]
    width = rows.shape[1]
    query_count = slot_count // parts
    query_unit = lax.dynamic_index_in_dim(
        unit_rows.reshape(query_count, parts, width), half, 1, keepdims=False
    )
    query_pos = parts * jnp.arange(query_count, dtype=jnp.int32)
    query_block = pick_block(query_count, 512)
    block_unit = query_unit
    block_pos = query_pos

    def compute(unused, block_unit=block_unit, block_pos=block_pos):
        return key_sweep(
            block_unit, block_pos, unit_rows, packed, packed_weight, exponent_sharpness, live_count
        )

    def nothing(unused):
        return (
            jnp.zeros((query_block,), jnp.float32),
            jnp.zeros((query_block, width), jnp.float32),
        )

    totals, numer = lax.cond(block_pos[0] < live_count, compute, nothing, 0)
    smooth_partial, score_part = finish(totals, numer, exponent_sharpness)
    return (smooth_partial, score_part, perm)


def unpack(perm, smooth_rows, score_rows):
    back_rows = jnp.dot(perm, smooth_rows, preferred_element_type=jnp.float32).astype(jnp.bfloat16)
    back_score = jnp.dot(perm, score_rows[:, None], preferred_element_type=jnp.float32)[
        :, 0
    ].astype(jnp.bfloat16)
    return (back_rows, back_score)


def local(sentence_vectors, group_assignment, adjacent_importance, group_sharpness):
    devices = lax.axis_size("own")
    local_entries = group_sharpness.shape[0]
    row_count = sentence_vectors.shape[0]
    width = sentence_vectors.shape[1]
    capacity = max(2, 2 * row_count // (local_entries * devices))
    slot_count = devices * capacity
    ident = group_assignment[:, 0]
    ranked = block_ranks(ident)
    owner = ident // local_entries
    member_of = ident % local_entries
    slot_index = member_of * slot_count + owner * capacity + ranked
    all_slots = jnp.arange(local_entries * slot_count, dtype=jnp.int32)
    onehot = (slot_index[:, None] == all_slots[None, :]).astype(jnp.bfloat16)
    send_rows = place_rows(onehot, sentence_vectors)
    send_weight = place_rows(onehot, adjacent_importance[:, None])[:, 0]
    got_rows, got_weight = (
        lax.all_to_all(
            send_rows.reshape(local_entries, devices, capacity, width),
            "own",
            split_axis=1,
            concat_axis=1,
            tiled=True,
        ),
        lax.all_to_all(
            send_weight.reshape(local_entries, devices, capacity),
            "own",
            split_axis=1,
            concat_axis=1,
            tiled=True,
        ),
    )
    got_rows = got_rows.reshape(local_entries, slot_count, width)
    got_weight = got_weight.reshape(local_entries, slot_count)
    smooth_list = []
    score_list = []
    for belongs_indicator in range(local_entries):
        smooth_partial, score_part, perm = cluster_share(
            got_rows[belongs_indicator],
            got_weight[belongs_indicator],
            group_sharpness[belongs_indicator].astype(jnp.float32),
            jnp.int32(0),
            1,
        )
        rows_home, score_home = unpack(perm, smooth_partial, score_part)
        smooth_list.append(rows_home)
        score_list.append(score_home)
    smooth_done = jnp.stack(smooth_list)
    score_done = jnp.stack(score_list)
    home_smooth, home_score = (
        lax.all_to_all(
            smooth_done.reshape(local_entries, devices, capacity, width),
            "own",
            split_axis=1,
            concat_axis=1,
            tiled=True,
        ),
        lax.all_to_all(
            score_done.reshape(local_entries, devices, capacity),
            "own",
            split_axis=1,
            concat_axis=1,
            tiled=True,
        ),
    )
    smoothed = jnp.dot(
        onehot,
        home_smooth.reshape(local_entries * slot_count, width),
        preferred_element_type=jnp.float32,
    ).astype(jnp.bfloat16)
    dup_score = jnp.dot(
        onehot,
        home_score.reshape(local_entries * slot_count, 1),
        preferred_element_type=jnp.float32,
    )[:, 0].astype(jnp.bfloat16)
    return (smoothed, dup_score)


def solution(mesh):
    placed = (P("own", None), P("own", None), P("own"), P("own"))
    return jax.shard_map(
        local, mesh=mesh, in_specs=placed, out_specs=(P("own", None), P("own")), check_vma=False
    )
```

profile of v0, /device:TPU:1, one launch (start us, length us, event | category | flops | bytes accessed | tf_op | source)
XLA Modules:
  0.0 164.0 jit_solution(14007054979766578386)
XLA Ops:
  3.9 1.5 copy.31
  5.4 11.5 %all-to-all-start = ((bf16[4,128,2]{0,2,1:T(2,128)(2,1)}), bf16[4,128,2]{0,2,1:T(2,128)(2,1)S(1)}, u32[]{:S(2)}, u32[]{:S(2)}) async-start(bf16[4,128,2]{0,2,1:T(2,128)(2,1)} %copy.31), calls=%async_computation | async-start | bytes 131072 | tf_op jit(solution)/shard_map/all_to_all | solution.py:148
  16.9 2.7 %fusion.28 = bf16[1024,1024]{1,0:T(8,128)(2,1)} fusion(bf16[512,1024]{1,0:T(8,128)(2,1)S(1)} %copy-done, s32[512]{0:T(512)S(1)} %bitcast.74), kind=kOutput, calls=%fused_computation.38 | convolution fusion | flops 1075314688 | bytes 3147776 | tf_op jit(solution)/shard_map/dot_general | solution.py:28
  23.4 2.8 %reshape.280 = bf16[4,128,2,1024]{3,2,1,0:T(2,128)(2,1)S(1)} reshape(bf16[1024,1024]{1,0:T(8,128)(2,1)} %fusion.28) | data formatting | bytes 4194304 | tf_op jit(solution)/shard_map/reshape | solution.py:142
  26.1 3.7 %copy.32 = bf16[4,128,2,1024]{3,2,0,1:T(2,128)(2,1)} copy(bf16[4,128,2,1024]{3,2,1,0:T(2,128)(2,1)S(1)} %reshape.280) | data formatting | bytes 4194304 | tf_op jit(solution)/shard_map/reshape | solution.py:142
  29.9 9.8 %all-to-all-start.1 = ((bf16[4,128,2,1024]{3,2,0,1:T(2,128)(2,1)}), bf16[4,128,2,1024]{3,2,0,1:T(2,128)(2,1)S(1)}, u32[]{:S(2)}, u32[]{:S(2)}) async-start(bf16[4,128,2,1024]{3,2,0,1:T(2,128)(2,1)} %copy.32), calls=%async_computation.1 | async-start | bytes 4194304 | tf_op jit(solution)/shard_map/all_to_all | solution.py:141
  50.2 1.4 compare_select_fusion.5
  52.0 17.7 %all-to-all-done.1 = bf16[4,128,2,1024]{3,2,0,1:T(2,128)(2,1)S(1)} async-done(((bf16[4,128,2,1024]{3,2,0,1:T(2,128)(2,1)}), bf16[4,128,2,1024]{3,2,0,1:T(2,128)(2,1)S(1)}, u32[]{:S(2)}, u32[]{:S(2)}) %all-to-all-start.1) | async-done | bytes 2097184 | tf_op jit(solution)/shard_map/all_to_all | solution.py:141
  69.8 2.8 %fusion.86 = (bf16[1,128,2,1024]{3,2,0,1:T(2,128)(2,1)}, bf16[1,128,2,1024]{3,2,0,1:T(2,128)(2,1)}, bf16[1,128,2,1024]{3,2,0,1:T(2,128)(2,1)}, bf16[1,128,2,1024]{3,2,0,1:T(2,128)(2,1)}) fusion(bf16[4,128,2,1024]{3,2,0,1:T(2,128)(2,1)S(1)} %all-to-all-done.1), kind=kLoop, calls=%fused_computation.165 | loop fusion | bytes 4194304 | tf_op jit(solution)/shard_map/slice | solution.py:162
  74.5 3.0 %conditional.8 = ((f32[256]{0:T(256)}, f32[256,1024]{1,0:T(8,128)})) conditional(s32[]{:T(128)} %convert_element_type.301, () %tuple.68, (s32[]{:T(128)}, bf16[256]{0:T(256)(128)(2,1)S(1)}, f32[]{:T(128)}, s32[256]{0:T(256)S(1)}, bf16[256,1024]{1,0:T(8,128)(2,1)S(1)}, /*index=5*/bf16[256,1024]{1,0:T(8,128)(2,1)S(1)}) %tuple.69), branch_computations={%region_4.5_spmd, %region_5.9_spmd} | conditional | flops 268894208 | bytes 2363986 | solution.py:111
  75.3 2.3 %conditional = (f32[256]{0:T(256)}, f32[256,1024]{1,0:T(8,128)}) conditional(s32[]{:T(128)} %convert_element_type.226, () %tuple.41, (bf16[256]{0:T(256)(128)(2,1)S(1)}, f32[]{:T(128)}, s32[256]{0:T(256)S(1)}, bf16[256,1024]{1,0:T(8,128)(2,1)S(1)}, bf16[256,1024]{1,0:T(8,128)(2,1)S(1)}) %tuple.42), branch_computations={%region_6.6_spmd, %region_7.8_spmd} | conditional | flops 268894208 | bytes 2363924 | solution.py:68
  76.2 1.3 fusion.4
  79.8 3.0 %conditional.11 = ((f32[256]{0:T(256)}, f32[256,1024]{1,0:T(8,128)})) conditional(s32[]{:T(128)} %convert_element_type.335, () %tuple.74, (s32[]{:T(128)}, bf16[256]{0:T(256)(128)(2,1)S(1)}, f32[]{:T(128)}, s32[256]{0:T(256)S(1)}, bf16[256,1024]{1,0:T(8,128)(2,1)S(1)}, /*index=5*/bf16[256,1024]{1,0:T(8,128)(2,1)S(1)}) %tuple.75), branch_computations={%region_28.29_spmd, %region_29.33_spmd} | conditional | flops 268894208 | bytes 2363986 | solution.py:111
  80.6 2.3 %conditional.3 = (f32[256]{0:T(256)}, f32[256,1024]{1,0:T(8,128)}) conditional(s32[]{:T(128)} %convert_element_type.235, () %tuple.56, (bf16[256]{0:T(256)(128)(2,1)S(1)}, f32[]{:T(128)}, s32[256]{0:T(256)S(1)}, bf16[256,1024]{1,0:T(8,128)(2,1)S(1)}, bf16[256,1024]{1,0:T(8,128)(2,1)S(1)}) %tuple.57), branch_computations={%region_30.30_spmd, %region_31.32_spmd} | conditional | flops 268894208 | bytes 2363924 | solution.py:68
  85.1 2.9 %conditional.10 = ((f32[256]{0:T(256)}, f32[256,1024]{1,0:T(8,128)})) conditional(s32[]{:T(128)} %convert_element_type.324, () %tuple.72, (s32[]{:T(128)}, bf16[256]{0:T(256)(128)(2,1)S(1)}, f32[]{:T(128)}, s32[256]{0:T(256)S(1)}, bf16[256,1024]{1,0:T(8,128)(2,1)S(1)}, /*index=5*/bf16[256,1024]{1,0:T(8,128)(2,1)S(1)}) %tuple.73), branch_computations={%region_20.21_spmd, %region_21.25_spmd} | conditional | flops 268894208 | bytes 2363986 | solution.py:111
  85.8 2.3 %conditional.2 = (f32[256]{0:T(256)}, f32[256,1024]{1,0:T(8,128)}) conditional(s32[]{:T(128)} %convert_element_type.232, () %tuple.51, (bf16[256]{0:T(256)(128)(2,1)S(1)}, f32[]{:T(128)}, s32[256]{0:T(256)S(1)}, bf16[256,1024]{1,0:T(8,128)(2,1)S(1)}, bf16[256,1024]{1,0:T(8,128)(2,1)S(1)}) %tuple.52), branch_computations={%region_22.22_spmd, %region_23.24_spmd} | conditional | flops 268894208 | bytes 2363924 | solution.py:68
  90.3 3.0 %conditional.9 = ((f32[256]{0:T(256)}, f32[256,1024]{1,0:T(8,128)})) conditional(s32[]{:T(128)} %convert_element_type.313, () %tuple.70, (s32[]{:T(128)}, bf16[256]{0:T(256)(128)(2,1)S(1)}, f32[]{:T(128)}, s32[256]{0:T(256)S(1)}, bf16[256,1024]{1,0:T(8,128)(2,1)S(1)}, /*index=5*/bf16[256,1024]{1,0:T(8,128)(2,1)S(1)}) %tuple.71), branch_computations={%region_12.13_spmd, %region_13.17_spmd} | conditional | flops 268894208 | bytes 2363986 | solution.py:111
  91.0 2.3 %conditional.1 = (f32[256]{0:T(256)}, f32[256,1024]{1,0:T(8,128)}) conditional(s32[]{:T(128)} %convert_element_type.229, () %tuple.46, (bf16[256]{0:T(256)(128)(2,1)S(1)}, f32[]{:T(128)}, s32[256]{0:T(256)S(1)}, bf16[256,1024]{1,0:T(8,128)(2,1)S(1)}, bf16[256,1024]{1,0:T(8,128)(2,1)S(1)}) %tuple.47), branch_computations={%region_14.14_spmd, %region_15.16_spmd} | conditional | flops 268894208 | bytes 2363924 | solution.py:68
  92.0 1.4 fusion.10
  94.7 1.6 %convolution_convert_fusion.6 = bf16[256,1024]{1,0:T(8,128)(2,1)S(1)} fusion(f32[256,1024]{1,0:T(8,128)} %get-tuple-element.151, f32[256]{0:T(256)S(1)} %get-tuple-element.179, pred[256]{0:T(512)(128)(4,1)S(1)} %broadcast_compare_fusion.3, s32[256]{0:T(256)S(1)} %get-tuple-element.201), kind=kOutput, calls=%fused_computation.54 | convolution fusion | flops 135331840 | bytes 1575168 | tf_op jit(solution)/shard_map/dot_general | solution.py:117
  97.0 1.6 convolution_convert_fusion
  99.3 1.6 %convolution_convert_fusion.2 = bf16[256,1024]{1,0:T(8,128)(2,1)S(1)} fusion(f32[256,1024]{1,0:T(8,128)} %get-tuple-element.155, f32[256]{0:T(256)S(1)} %get-tuple-element.183, pred[256]{0:T(512)(128)(4,1)S(1)} %broadcast_compare_fusion.1, s32[256]{0:T(256)S(1)} %get-tuple-element.199), kind=kOutput, calls=%fused_computation.50 | convolution fusion | flops 135331840 | bytes 1575168 | tf_op jit(solution)/shard_map/dot_general | solution.py:117
  101.6 2.4 %convolution_convert_fusion.4 = bf16[256,1024]{1,0:T(8,128)(2,1)} fusion(f32[256,1024]{1,0:T(8,128)} %get-tuple-element.153, f32[256]{0:T(256)S(1)} %get-tuple-element.181, pred[256]{0:T(512)(128)(4,1)S(1)} %broadcast_compare_fusion.2, s32[256]{0:T(256)S(1)} %get-tuple-element.200), kind=kOutput, calls=%fused_computation.52 | convolution fusion | flops 135331840 | bytes 1575168 | tf_op jit(solution)/shard_map/dot_general | solution.py:117
  105.7 1.5 copy.38
  107.2 4.7 %all-to-all-start.3 = ((bf16[4,128,2]{0,2,1:T(2,128)(2,1)}), bf16[4,128,2]{0,2,1:T(2,128)(2,1)S(1)}, u32[]{:S(2)}, u32[]{:S(2)}) async-start(bf16[4,128,2]{0,2,1:T(2,128)(2,1)} %copy.38), calls=%async_computation.3 | async-start | bytes 131072 | tf_op jit(solution)/shard_map/all_to_all | solution.py:181
  111.9 4.0 %pad_maximum_fusion = bf16[4,128,2,1024]{3,2,0,1:T(2,128)(2,1)} fusion(bf16[1,128,2,1024]{3,2,0,1:T(2,128)(2,1)S(1)} %bitcast.67, bf16[1,128,2,1024]{3,2,0,1:T(2,128)(2,1)S(1)} %bitcast.68, bf16[1,128,2,1024]{3,2,0,1:T(2,128)(2,1)S(1)} %bitcast.69, bf16[1,128,2,1024]{3,2,0,1:T(2,128)(2,1)S(1)} %bitcast.66), kind=kLoop, calls=%fused_computation.32 | loop fusion | flops 3145728 | bytes 4194304 | tf_op jit(solution)/shard_map/stack | solution.py:171
  115.9 5.7 %all-to-all-done.3 = bf16[4,128,2]{0,2,1:T(2,128)(2,1)S(1)} async-done(((bf16[4,128,2]{0,2,1:T(2,128)(2,1)}), bf16[4,128,2]{0,2,1:T(2,128)(2,1)S(1)}, u32[]{:S(2)}, u32[]{:S(2)}) %all-to-all-start.3) | async-done | bytes 2080 | tf_op jit(solution)/shard_map/all_to_all | solution.py:181
  121.6 4.4 %all-to-all-start.2 = ((bf16[4,128,2,1024]{3,2,0,1:T(2,128)(2,1)}), bf16[4,128,2,1024]{3,2,0,1:T(2,128)(2,1)S(1)}, u32[]{:S(2)}, u32[]{:S(2)}) async-start(bf16[4,128,2,1024]{3,2,0,1:T(2,128)(2,1)} %pad_maximum_fusion), calls=%async_computation.2 | async-start | bytes 4194304 | tf_op jit(solution)/shard_map/all_to_all | solution.py:174
  128.4 27.8 %all-to-all-done.2 = bf16[4,128,2,1024]{3,2,0,1:T(2,128)(2,1)S(1)} async-done(((bf16[4,128,2,1024]{3,2,0,1:T(2,128)(2,1)}), bf16[4,128,2,1024]{3,2,0,1:T(2,128)(2,1)S(1)}, u32[]{:S(2)}, u32[]{:S(2)}) %all-to-all-start.2) | async-done | bytes 2097184 | tf_op jit(solution)/shard_map/all_to_all | solution.py:174
  156.1 2.8 %copy.37 = bf16[4,128,2,1024]{3,2,1,0:T(2,128)(2,1)} copy(bf16[4,128,2,1024]{3,2,0,1:T(2,128)(2,1)S(1)} %all-to-all-done.2) | data formatting | bytes 4194304 | tf_op jit(solution)/shard_map/all_to_all | solution.py:174
  158.9 2.7 %reshape.281 = bf16[1024,1024]{1,0:T(8,128)(2,1)S(1)} reshape(bf16[4,128,2,1024]{3,2,1,0:T(2,128)(2,1)} %copy.37) | data formatting | bytes 4194304 | tf_op jit(solution)/shard_map/reshape | solution.py:191
  161.7 2.3 %fusion.29 = bf16[512,1024]{1,0:T(8,128)(2,1)} fusion(bf16[1024,1024]{1,0:T(8,128)(2,1)S(1)} %reshape.281, s32[512]{0:T(512)S(1)} %bitcast.76), kind=kOutput, calls=%fused_computation.39 | convolution fusion | flops 1074790400 | bytes 3147776 | tf_op jit(solution)/shard_map/dot_general | solution.py:189
  (110 shorter events, 32.5 us)
Async XLA Ops:
  0.6 16.3 %copy-start = (bf16[512,1024]{1,0:T(8,128)(2,1)S(1)}, bf16[512,1024]{1,0:T(8,128)(2,1)}, u32[]{:S(2)}) copy-start(bf16[512,1024]{1,0:T(8,128)(2,1)} %param.20) | copy-start | bytes 3145732
  5.4 24.5 %all-to-all-start = ((bf16[4,128,2]{0,2,1:T(2,128)(2,1)}), bf16[4,128,2]{0,2,1:T(2,128)(2,1)S(1)}, u32[]{:S(2)}, u32[]{:S(2)}) async-start(bf16[4,128,2]{0,2,1:T(2,128)(2,1)} %copy.31), calls=%async_computation | async-start | bytes 131072 | tf_op jit(solution)/shard_map/all_to_all | solution.py:148
  16.9 2.7 %copy-start.4 = (bf16[4]{0:T(256)(128)(2,1)S(1)}, bf16[4]{0:T(256)(128)(2,1)}, u32[]{:S(2)}) copy-start(bf16[4]{0:T(256)(128)(2,1)} %param.23) | copy-start | bytes 28
  29.9 39.9 %all-to-all-start.1 = ((bf16[4,128,2,1024]{3,2,0,1:T(2,128)(2,1)}), bf16[4,128,2,1024]{3,2,0,1:T(2,128)(2,1)S(1)}, u32[]{:S(2)}, u32[]{:S(2)}) async-start(bf16[4,128,2,1024]{3,2,0,1:T(2,128)(2,1)} %copy.32), calls=%async_computation.1 | async-start | bytes 4194304 | tf_op jit(solution)/shard_map/all_to_all | solution.py:141
  74.5 4.4 %copy-start.3 = (bf16[1,128,2,1024]{3,2,0,1:T(2,128)(2,1)S(1)}, bf16[1,128,2,1024]{3,2,0,1:T(2,128)(2,1)}, u32[]{:S(2)}) copy-start(bf16[1,128,2,1024]{3,2,0,1:T(2,128)(2,1)} %get-tuple-element.175) | copy-start | bytes 1572868
  79.8 4.4 %copy-start.2 = (bf16[1,128,2,1024]{3,2,0,1:T(2,128)(2,1)S(1)}, bf16[1,128,2,1024]{3,2,0,1:T(2,128)(2,1)}, u32[]{:S(2)}) copy-start(bf16[1,128,2,1024]{3,2,0,1:T(2,128)(2,1)} %get-tuple-element.176) | copy-start | bytes 1572868
  85.1 4.3 %copy-start.1 = (bf16[1,128,2,1024]{3,2,0,1:T(2,128)(2,1)S(1)}, bf16[1,128,2,1024]{3,2,0,1:T(2,128)(2,1)}, u32[]{:S(2)}) copy-start(bf16[1,128,2,1024]{3,2,0,1:T(2,128)(2,1)} %get-tuple-element.177) | copy-start | bytes 1572868
  107.2 14.4 %all-to-all-start.3 = ((bf16[4,128,2]{0,2,1:T(2,128)(2,1)}), bf16[4,128,2]{0,2,1:T(2,128)(2,1)S(1)}, u32[]{:S(2)}, u32[]{:S(2)}) async-start(bf16[4,128,2]{0,2,1:T(2,128)(2,1)} %copy.38), calls=%async_computation.3 | async-start | bytes 131072 | tf_op jit(solution)/shard_map/all_to_all | solution.py:181
  121.6 34.5 %all-to-all-start.2 = ((bf16[4,128,2,1024]{3,2,0,1:T(2,128)(2,1)}), bf16[4,128,2,1024]{3,2,0,1:T(2,128)(2,1)S(1)}, u32[]{:S(2)}, u32[]{:S(2)}) async-start(bf16[4,128,2,1024]{3,2,0,1:T(2,128)(2,1)} %pad_maximum_fusion), calls=%async_computation.2 | async-start | bytes 4194304 | tf_op jit(solution)/shard_map/all_to_all | solution.py:174
where the time goes:
time: 165 us; the launch traced here: 164 us
  waiting for transfers between devices  51.2 us (31%)
  starting transfers between devices  30.3 us (18%)
  local copies, waits for them, and re-layouts  27.8 us (17%)
  matrix products  26.2 us (16%)
  other arithmetic  16.8 us (10%)
  between operations  8.69 us (5%)
  loops' own time  2.98 us (2%)
    all_to_all x1, waiting for transfers between devices, local(): lax.all_to_all(smooth_done.reshape(local_entries, devices, capacity, widt...  27.8 us
    all_to_all x1, waiting for transfers between devices, local(): lax.all_to_all(send_rows.reshape(local_entries, devices, capacity, width)...  17.7 us
    all_to_all x1, starting transfers between devices, local(): lax.all_to_all(send_weight.reshape(local_entries, devices, capacity), 'ow...  11.5 us
    all_to_all x1, starting transfers between devices, local(): lax.all_to_all(send_rows.reshape(local_entries, devices, capacity, width)...  9.76 us
    dot_general x4, matrix products, unpack(): jnp.dot(perm, smooth_rows, preferred_element_type=jnp.float32)  7.36 us
    reshape x2, local copies, waits for them, and re-layouts, local(): send_rows.reshape(local_entries, devices, capacity, width)  6.5 us
    dot_general x10, matrix products, place_rows(): lax.dot_general(onehot, values, (((0,), (0,)), ((), ())), preferred_eleme...  6.1 us
    all_to_all x1, waiting for transfers between devices, local(): lax.all_to_all(score_done.reshape(local_entries, devices, capacity), 'own...  5.7 us
  transfers between devices with their start and end apart: 4, of which 3 were waited for; matrix products, arithmetic and copies ran while one was open for 15% of the time, Pallas kernels for 0%

commit v1 on v0

v1 whole, which is shorter than its diff:
```python
import jax
import jax.numpy as jnp
from jax import lax
from jax.experimental import pallas as pl
from jax.experimental.pallas import tpu as pltpu
from jax.sharding import PartitionSpec as P

F32 = jnp.float32
BF16 = jnp.bfloat16
LANES = 128
CAP = 2


def iota(shape, dim):
    return lax.broadcasted_iota(jnp.int32, shape, dim)


def column_of(row):
    count = row.shape[1]
    parts = []
    for start in range(0, count, LANES):
        wide = jnp.broadcast_to(row[:, start : start + LANES], (LANES, LANES))
        parts.append(jnp.transpose(wide))
    return jnp.concatenate(parts, axis=0)


def row_of(column):
    count = column.shape[0]
    parts = []
    for start in range(0, count, LANES):
        parts.append(jnp.transpose(column[start : start + LANES, :])[0:1, :])
    return jnp.concatenate(parts, axis=1)


def dot(a, b, contract=((1,), (0,))):
    return lax.dot_general(a, b, (contract, ((), ())), preferred_element_type=F32)


def pack_kernel(ident_ref, weight_ref, rows_ref, send_ref, slot_ref):
    count = rows_ref.shape[0]
    width = rows_ref.shape[1]
    slots = send_ref.shape[0]
    ident = ident_ref[...]
    ident_col = column_of(ident)
    ranks = []
    for start in range(0, count, LANES):
        here = ident[:, start : start + LANES]
        same = ident_col == here
        earlier = iota((count, LANES), 0) < iota((count, LANES), 1) + start
        ranks.append(jnp.sum((same & earlier).astype(jnp.int32), axis=0, keepdims=True))
    slot = CAP * ident + jnp.concatenate(ranks, axis=1)
    slot_ref[...] = slot
    weight_col = column_of(weight_ref[...].astype(F32)).astype(BF16)
    block = 256

    for index in range(slots // block):
        start = index * block
        hot = (slot == start + iota((block, count), 0)).astype(BF16)
        send_ref[start : start + block, 0:width] = dot(hot, rows_ref[...]).astype(BF16)
        send_ref[start : start + block, width : width + LANES] = dot(hot, weight_col).astype(BF16)


def pack(ident, weight, rows, slots):
    count, width = rows.shape
    vmem = pl.BlockSpec(memory_space=pltpu.VMEM)
    return pl.pallas_call(
        pack_kernel,
        out_shape=(
            jax.ShapeDtypeStruct((slots, width + LANES), BF16),
            jax.ShapeDtypeStruct((1, count), jnp.int32),
        ),
        in_specs=[vmem] * 3,
        out_specs=(vmem, vmem),
        cost_estimate=pl.CostEstimate(
            flops=2 * slots * count * (width + LANES), bytes_accessed=4 << 20, transcendentals=0
        ),
        compiler_params=pltpu.CompilerParams(vmem_limit_bytes=12 << 20),
        name="pack",
    )(ident, weight, rows)


def hot_kernel(slot_ref, hot_ref):
    count, slots = hot_ref.shape
    slot_col = column_of(slot_ref[...])
    for start in range(0, slots, LANES):
        hot_ref[:, start : start + LANES] = (slot_col == start + iota((count, LANES), 1)).astype(BF16)


def hot_rows(slot, slots):
    count = slot.shape[1]
    vmem = pl.BlockSpec(memory_space=pltpu.VMEM)
    return pl.pallas_call(
        hot_kernel,
        out_shape=jax.ShapeDtypeStruct((count, slots), BF16),
        in_specs=[vmem],
        out_specs=vmem,
        cost_estimate=pl.CostEstimate(flops=count * slots, bytes_accessed=1 << 20, transcendentals=0),
        compiler_params=pltpu.CompilerParams(vmem_limit_bytes=8 << 20),
        name="hot_rows",
    )(slot)


def cluster_kernel(sharp_ref, got_ref, back_ref, rows_s, unit_s, weight_s, done_s):
    members = sharp_ref.shape[1]
    slots, wide = got_ref.shape
    width = wide - LANES
    block = 256
    share = members * CAP
    group = block // members
    new, old = iota((block, block), 0), iota((block, block), 1)
    from_old = (new % group) // CAP * share + new // group * CAP + new % CAP
    perm = (from_old == old).astype(BF16)
    from_new = (old % group) // CAP * share + old // group * CAP + old % CAP
    unperm = (from_new == new).astype(BF16)

    for index in range(slots // block):
        taken = got_ref[index * block : (index + 1) * block, :]
        moved = dot(perm, taken[:, 0:width])
        weight = dot(perm, taken[:, width:wide])
        square_sum = jnp.sum(moved * moved, axis=1, keepdims=True)
        unit = (moved * lax.rsqrt(square_sum + 1e-06)).astype(BF16)
        moved = moved.astype(BF16)
        for member in range(members):
            at = member * slots // members + index * group
            of = slice(member * group, (member + 1) * group)
            rows_s[at : at + group, :] = moved[of, :]
            unit_s[at : at + group, :] = unit[of, :]
            weight_s[at : at + group, :] = weight[of, :]

    each = slots // members
    same = iota((each, each), 0) == iota((each, each), 1)
    for member in range(members):
        of = slice(member * each, (member + 1) * each)
        sharp = sharp_ref[0, member]
        unit = unit_s[of, :]
        cosine = jnp.where(same, F32(0.0), dot(unit, unit, ((1,), (1,))))
        expo = row_of(weight_s[of, :]) * jnp.exp(sharp * (cosine - 1.0))
        total = jnp.sum(expo, axis=1, keepdims=True)
        numer = dot(expo.astype(BF16), rows_s[of, :])
        done_s[of, 0:width] = (numer * (1.0 / total)).astype(BF16)
        score = (jnp.log(total) + sharp).astype(BF16)
        done_s[of, width:wide] = jnp.broadcast_to(score, (each, LANES))

    for index in range(slots // block):
        parts = []
        for member in range(members):
            at = member * each + index * group
            parts.append(done_s[at : at + group, :])
        done = jnp.concatenate(parts, axis=0)
        back_ref[index * block : (index + 1) * block, :] = dot(unperm, done).astype(BF16)


def clusters(sharp, got):
    slots, wide = got.shape
    vmem = pl.BlockSpec(memory_space=pltpu.VMEM)
    return pl.pallas_call(
        cluster_kernel,
        out_shape=jax.ShapeDtypeStruct((slots, wide), BF16),
        in_specs=[pl.BlockSpec(memory_space=pltpu.SMEM), vmem],
        out_specs=vmem,
        scratch_shapes=[
            pltpu.VMEM((slots, wide - LANES), BF16),
            pltpu.VMEM((slots, wide - LANES), BF16),
            pltpu.VMEM((slots, LANES), F32),
            pltpu.VMEM((slots, wide), BF16),
        ],
        compiler_params=pltpu.CompilerParams(vmem_limit_bytes=20 << 20),
        name="clusters",
    )(sharp, got)


def home_kernel(hot_ref, home_ref, smooth_ref, score_ref):
    count, width = smooth_ref.shape
    block = 256
    for start in range(0, count, block):
        hot = hot_ref[start : start + block, :]
        smooth_ref[start : start + block, :] = dot(hot, home_ref[:, 0:width]).astype(BF16)
        score = row_of(dot(hot, home_ref[:, width : width + LANES]))
        score_ref[:, start : start + block] = score.astype(BF16)


def bring_home(hot, home):
    count = hot.shape[0]
    width = home.shape[1] - LANES
    vmem = pl.BlockSpec(memory_space=pltpu.VMEM)
    return pl.pallas_call(
        home_kernel,
        out_shape=(
            jax.ShapeDtypeStruct((count, width), BF16),
            jax.ShapeDtypeStruct((1, count), BF16),
        ),
        in_specs=[vmem] * 2,
        out_specs=(vmem, vmem),
        compiler_params=pltpu.CompilerParams(vmem_limit_bytes=12 << 20),
        name="bring_home",
    )(hot, home)


def local(sentence_vectors, group_assignment, adjacent_importance, group_sharpness):
    devices = lax.axis_size("own")
    local_entries = group_sharpness.shape[0]
    row_count = sentence_vectors.shape[0]
    slots = devices * local_entries * CAP
    send, slot = pack(
        group_assignment.reshape(1, row_count),
        adjacent_importance.reshape(1, row_count),
        sentence_vectors,
        slots,
    )
    got = lax.all_to_all(send, "own", split_axis=0, concat_axis=0, tiled=True)
    sharp = group_sharpness.astype(F32).reshape(1, local_entries)
    back = clusters(sharp, got)
    hot = hot_rows(slot, slots)
    home = lax.all_to_all(back, "own", split_axis=0, concat_axis=0, tiled=True)
    smoothed, score = bring_home(hot, home)
    return (smoothed, score.reshape(row_count))


def solution(mesh):
    placed = (P("own", None), P("own", None), P("own"), P("own"))
    return jax.shard_map(
        local, mesh=mesh, in_specs=placed, out_specs=(P("own", None), P("own")), check_vma=False
    )
```

time: 165 us -> 97 us (0.59)
  matrix products: 26.2 us -> 0 us
  local copies, waits for them, and re-layouts: 27.8 us -> 5.41 us
  other arithmetic: 16.8 us -> 0.58 us
  waiting for transfers between devices: 51.2 us -> 65.7 us
  starting transfers between devices: 30.3 us -> 16.2 us
  Pallas kernels: 0 us -> 8.09 us
  between operations: 8.69 us -> 0.7 us
  loops' own time: 2.98 us -> 0 us
    dot_general x28 -> x0, matrix products: 26.2 us -> none  [the longest x4 7.36 us: unpack(): jnp.dot(perm, smooth_rows, preferred_element_type=jnp.float32)]
    all_to_all x4 -> x2, waiting for transfers between devices: 51.2 us -> 65.7 us  [the longest x1 32.9 us: local(): got = lax.all_to_all(send, 'own', split_axis=0, concat_axis=0, tiled=True)]
    all_to_all x4 -> x2, starting transfers between devices: 30.3 us -> 16.2 us  [the longest x1 11.5 us: local(): got = lax.all_to_all(send, 'own', split_axis=0, concat_axis=0, tiled=True)]
    reshape x3 -> x1, local copies, waits for them, and re-layouts: 9.24 us -> 0.68 us  [local(): adjacent_importance.reshape(1, row_count)]
    pallas_call x0 -> x4, Pallas kernels: none -> 8.09 us  [the longest x1 3.76 us: clusters(): pl.pallas_call(cluster_kernel, out_shape=jax.ShapeDtypeStruct((slots, wid...]
    another operation x8 -> x0, local copies, waits for them, and re-layouts: 5.3 us -> none  [the longest x4 1.83 us: local(): smooth_done = jnp.stack(smooth_list)]
    slice x4 -> x0, local copies, waits for them, and re-layouts: 4.87 us -> none  [the longest x1 2.8 us: local(): got_rows[belongs_indicator]]
    convert_element_type x26 -> x0, other arithmetic: 4.06 us -> none  [the longest x4 2.74 us: finish(): jnp.where(positive, jnp.log(safe) + exponent_sharpness, jnp.float32(0.0))]
  transfers between devices with their start and end apart: 4 -> 2, of which waited for: 3 -> 2; matrix products, arithmetic and copies ran while one was open for 15% -> 0% of each run, Pallas kernels for 0% -> 0%
where the time goes in v1:
time: 97 us; the launch traced here: 96.7 us
  waiting for transfers between devices  65.7 us (68%)
  starting transfers between devices  16.2 us (17%)
  Pallas kernels  8.09 us (8%)
  local copies, waits for them, and re-layouts  5.41 us (6%)
    all_to_all x1, waiting for transfers between devices, local(): got = lax.all_to_all(send, 'own', split_axis=0, concat_axis=0, tiled=True)  32.9 us
    all_to_all x1, waiting for transfers between devices, local(): home = lax.all_to_all(back, 'own', split_axis=0, concat_axis=0, tiled=True)  32.8 us
    all_to_all x1, starting transfers between devices, local(): got = lax.all_to_all(send, 'own', split_axis=0, concat_axis=0, tiled=True)  11.5 us
    unnamed x10, local copies, waits for them, and re-layouts  4.73 us
    all_to_all x1, starting transfers between devices, local(): home = lax.all_to_all(back, 'own', split_axis=0, concat_axis=0, tiled=True)  4.73 us
    pallas_call x1, Pallas kernels, clusters(): pl.pallas_call(cluster_kernel, out_shape=jax.ShapeDtypeStruct((slots, wid...  3.76 us
    pallas_call x1, Pallas kernels, bring_home(): pl.pallas_call(home_kernel, out_shape=(jax.ShapeDtypeStruct((count, width...  2.36 us
  transfers between devices with their start and end apart: 2, of which 2 were waited for; matrix products, arithmetic and copies ran while one was open for 0% of the time, Pallas kernels for 0%

profile of v1, /device:TPU:1, one launch (start us, length us, event | category | flops | bytes accessed | tf_op | source)
XLA Modules:
  0.0 96.7 jit_solution(10039067785231863542)
XLA Ops:
  0.6 0.7 reshape.23.weight_ref
  1.3 0.0 copy-start.2
  1.3 1.2 %copy-done.2 = bf16[512,1024]{1,0:T(8,128)(2,1)S(1)} copy-done((bf16[512,1024]{1,0:T(8,128)(2,1)S(1)}, bf16[512,1024]{1,0:T(8,128)(2,1)}, u32[]{:S(2)}) %copy-start.2) | copy-done | bytes 1048600
  2.5 0.0 copy-start.3
  2.5 0.7 copy-done.3
  3.2 1.7 %pack.1 = (bf16[1024,1152]{1,0:T(8,128)(2,1)S(1)}, s32[1,512]{1,0:T(1,128)S(1)}) custom-call(s32[1,512]{1,0:T(1,128)S(1)} %bitcast.12, bf16[1,512]{1,0:T(2,128)(2,1)S(1)} %reshape.23.weight_ref, bf16[512,1024]{1,0:T(8,128)(2,1)S(1)} %copy-done.2), custom_call_target="tpu_custom_call" | custom-call | flops 1207959552 | bytes 4194304 | tf_op jit(solution)/shard_map/pack/pallas_call | solution.py:66
  4.9 0.0 copy-start.1
  4.9 1.4 %copy-done.1 = bf16[1024,1152]{1,0:T(8,128)(2,1)} copy-done((bf16[1024,1152]{1,0:T(8,128)(2,1)}, bf16[1024,1152]{1,0:T(8,128)(2,1)S(1)}, u32[]{:S(2)}) %copy-start.1) | copy-done | bytes 2359320
  6.3 0.0 copy-start.4
  6.3 11.5 %all-to-all-start = ((bf16[128,8,1152]{2,1,0:T(8,128)(2,1)}), bf16[128,8,1152]{2,1,0:T(8,128)(2,1)S(1)}, u32[]{:S(2)}, u32[]{:S(2)}) async-start(bf16[128,8,1152]{2,1,0:T(8,128)(2,1)} %bitcast.11), calls=%async_computation | async-start | bytes 4718592 | tf_op jit(solution)/shard_map/all_to_all | solution.py:210
  17.8 0.0 copy-done.4
  17.9 32.9 %all-to-all-done = bf16[128,8,1152]{2,1,0:T(8,128)(2,1)S(1)} async-done(((bf16[128,8,1152]{2,1,0:T(8,128)(2,1)}), bf16[128,8,1152]{2,1,0:T(8,128)(2,1)S(1)}, u32[]{:S(2)}, u32[]{:S(2)}) %all-to-all-start) | async-done | bytes 2359328 | tf_op jit(solution)/shard_map/all_to_all | solution.py:210
  50.8 3.8 %clusters.1 = bf16[1024,1152]{1,0:T(8,128)(2,1)S(1)} custom-call(f32[1,4]{1,0:T(1,128)S(1)} %bitcast_convert_fusion.sharp_ref, bf16[1024,1152]{1,0:T(8,128)(2,1)S(1)} %bitcast.9), custom_call_target="tpu_custom_call" | custom-call | tf_op jit(solution)/shard_map/clusters/pallas_call | solution.py:156
  54.5 0.0 copy-start
  54.5 1.4 %copy-done = bf16[1024,1152]{1,0:T(8,128)(2,1)} copy-done((bf16[1024,1152]{1,0:T(8,128)(2,1)}, bf16[1024,1152]{1,0:T(8,128)(2,1)S(1)}, u32[]{:S(2)}) %copy-start) | copy-done | bytes 2359320
  55.9 4.7 %all-to-all-start.1 = ((bf16[128,8,1152]{2,1,0:T(8,128)(2,1)}), bf16[128,8,1152]{2,1,0:T(8,128)(2,1)S(1)}, u32[]{:S(2)}, u32[]{:S(2)}) async-start(bf16[128,8,1152]{2,1,0:T(8,128)(2,1)} %bitcast.10), calls=%async_computation.1 | async-start | bytes 4718592 | tf_op jit(solution)/shard_map/all_to_all | solution.py:214
  60.7 0.3 hot_rows.1.hot_ref
  61.0 32.8 %all-to-all-done.1 = bf16[128,8,1152]{2,1,0:T(8,128)(2,1)S(1)} async-done(((bf16[128,8,1152]{2,1,0:T(8,128)(2,1)}), bf16[128,8,1152]{2,1,0:T(8,128)(2,1)S(1)}, u32[]{:S(2)}, u32[]{:S(2)}) %all-to-all-start.1) | async-done | bytes 2359328 | tf_op jit(solution)/shard_map/all_to_all | solution.py:214
  93.7 2.4 %bring_home.1 = (bf16[512,1024]{1,0:T(8,128)(2,1)}, bf16[1,512]{1,0:T(2,128)(2,1)S(1)}) custom-call(bf16[512,1024]{1,0:T(8,128)(2,1)S(1)} %hot_rows.1.hot_ref, bf16[1024,1152]{1,0:T(8,128)(2,1)S(1)} %bitcast.8), custom_call_target="tpu_custom_call" | custom-call | tf_op jit(solution)/shard_map/bring_home/pallas_call | solution.py:186
  96.1 0.6 reduce
  (1 shorter events, 0.0 us)
Async XLA Ops:
  1.3 1.2 %copy-start.2 = (bf16[512,1024]{1,0:T(8,128)(2,1)S(1)}, bf16[512,1024]{1,0:T(8,128)(2,1)}, u32[]{:S(2)}) copy-start(bf16[512,1024]{1,0:T(8,128)(2,1)} %rows_ref.1) | copy-start | bytes 3145732
  2.5 0.7 copy-start.3
  4.9 1.4 %copy-start.1 = (bf16[1024,1152]{1,0:T(8,128)(2,1)}, bf16[1024,1152]{1,0:T(8,128)(2,1)S(1)}, u32[]{:S(2)}) copy-start(bf16[1024,1152]{1,0:T(8,128)(2,1)S(1)} %get-tuple-element.7) | copy-start | bytes 7077892
  6.3 11.5 %copy-start.4 = (bf16[4]{0:T(256)(128)(2,1)S(1)}, bf16[4]{0:T(256)(128)(2,1)}, u32[]{:S(2)}) copy-start(bf16[4]{0:T(256)(128)(2,1)} %param.7) | copy-start | bytes 28
  6.3 44.4 %all-to-all-start = ((bf16[128,8,1152]{2,1,0:T(8,128)(2,1)}), bf16[128,8,1152]{2,1,0:T(8,128)(2,1)S(1)}, u32[]{:S(2)}, u32[]{:S(2)}) async-start(bf16[128,8,1152]{2,1,0:T(8,128)(2,1)} %bitcast.11), calls=%async_computation | async-start | bytes 4718592 | tf_op jit(solution)/shard_map/all_to_all | solution.py:210
  54.5 1.4 %copy-start = (bf16[1024,1152]{1,0:T(8,128)(2,1)}, bf16[1024,1152]{1,0:T(8,128)(2,1)S(1)}, u32[]{:S(2)}) copy-start(bf16[1024,1152]{1,0:T(8,128)(2,1)S(1)} %clusters.1) | copy-start | bytes 7077892
  55.9 37.8 %all-to-all-start.1 = ((bf16[128,8,1152]{2,1,0:T(8,128)(2,1)}), bf16[128,8,1152]{2,1,0:T(8,128)(2,1)S(1)}, u32[]{:S(2)}, u32[]{:S(2)}) async-start(bf16[128,8,1152]{2,1,0:T(8,128)(2,1)} %bitcast.10), calls=%async_computation.1 | async-start | bytes 4718592 | tf_op jit(solution)/shard_map/all_to_all | solution.py:214

commit v2 on v1

v2 whole, which is shorter than its diff:
```python
import jax
import jax.numpy as jnp
from jax import lax
from jax.experimental import pallas as pl
from jax.experimental.pallas import tpu as pltpu
from jax.sharding import PartitionSpec as P

F32 = jnp.float32
BF16 = jnp.bfloat16
LANES = 128
CAP = 2
BLOCK = 256
PARTS = 2
LOG2_E = 1.4426950408889634
MIB = 1 << 20
IN_VMEM = pl.BlockSpec(memory_space=pltpu.VMEM)
IN_SMEM = pl.BlockSpec(memory_space=pltpu.SMEM)
IN_HBM = pl.BlockSpec(memory_space=pltpu.HBM)


def iota(shape, dim):
    return lax.broadcasted_iota(jnp.int32, shape, dim)


def dot(a, b, contract=((1,), (0,))):
    return lax.dot_general(a, b, (contract, ((), ())), preferred_element_type=F32)


def column_of(row):
    parts = []
    for start in range(0, row.shape[1], LANES):
        wide = jnp.broadcast_to(row[:, start : start + LANES], (LANES, LANES))
        parts.append(jnp.transpose(wide))
    return jnp.concatenate(parts, axis=0)


def turned(tall):
    parts = []
    for start in range(0, tall.shape[0], LANES):
        parts.append(jnp.transpose(tall[start : start + LANES, :]))
    return jnp.concatenate(parts, axis=1)


def pack_kernel(
    members, ident_hbm, weight_hbm, rows_hbm, send_hbm, place_hbm, ident_s, weight_s, rows_s, place_s, send_s, sems
):
    count, width = rows_s.shape
    devices = send_s.shape[0]
    each = devices * CAP
    get_ident = pltpu.make_async_copy(ident_hbm, ident_s, sems.at[0])
    get_weight = pltpu.make_async_copy(weight_hbm, weight_s, sems.at[1])
    get_ident.start()
    get_weight.start()
    get_rows = []
    for index in range(PARTS):
        of = slice(index * count // PARTS, (index + 1) * count // PARTS)
        get_rows.append(pltpu.make_async_copy(rows_hbm.at[of, :], rows_s.at[of, :], sems.at[3 + index]))
        get_rows[-1].start()
    get_ident.wait()
    ident = ident_s[...]
    ident_col = column_of(ident)
    ranks = []
    for start in range(0, count, LANES):
        here = ident[:, start : start + LANES]
        same = ident_col == here
        earlier = iota((count, LANES), 0) < iota((count, LANES), 1) + start
        ranks.append(jnp.sum((same & earlier).astype(jnp.int32), axis=0, keepdims=True))
    member = ident % members
    within = ident // members * CAP + jnp.concatenate(ranks, axis=1)
    place = member * each + within
    place_s[0:1, :] = place
    place_s[1:2, :] = within
    place_s[2:3, :] = member
    put_place = pltpu.make_async_copy(place_s, place_hbm, sems.at[2])
    put_place.start()
    get_weight.wait()
    weight = weight_s[...].astype(F32).reshape(1, count)
    own_lane = iota((LANES, count), 0) == member
    weights = turned_back(jnp.where(own_lane, weight, F32(0.0))).astype(BF16)
    hot = (within == iota((each, count), 0)).astype(BF16)
    send_s[:, :, members * width :] = dot(hot, weights).astype(BF16).reshape(devices, CAP, LANES)
    for copy in get_rows:
        copy.wait()
    copies = []
    for index in range(members):
        hot = (place == index * each + iota((each, count), 0)).astype(BF16)
        packed = dot(hot, rows_s[...]).astype(BF16)
        first, last = index * width, (index + 1) * width
        send_s[:, :, first:last] = packed.reshape(devices, CAP, width)
        if index == members - 1:
            last = last + LANES
        copies.append(
            pltpu.make_async_copy(
                send_s.at[:, :, first:last], send_hbm.at[:, :, first:last], sems.at[3 + PARTS + index]
            )
        )
        copies[-1].start()
    put_place.wait()
    for copy in copies:
        copy.wait()


def turned_back(wide):
    parts = []
    for start in range(0, wide.shape[1], LANES):
        parts.append(jnp.transpose(wide[:, start : start + LANES]))
    return jnp.concatenate(parts, axis=0)


def pack(ident, weight, rows, devices, members):
    count, width = rows.shape
    wide = members * width + LANES

    def kernel(*refs):
        pack_kernel(members, *refs)

    return pl.pallas_call(
        kernel,
        out_shape=(
            pltpu.HBM((devices, CAP, wide), BF16),
            pltpu.HBM((3, count), jnp.int32),
        ),
        in_specs=[IN_HBM] * 3,
        out_specs=(IN_HBM, IN_HBM),
        scratch_shapes=[
            pltpu.VMEM((1, count), jnp.int32),
            pltpu.VMEM((count,), BF16),
            pltpu.VMEM((count, width), BF16),
            pltpu.VMEM((3, count), jnp.int32),
            pltpu.VMEM((devices, CAP, wide), BF16),
            pltpu.SemaphoreType.DMA((3 + PARTS + members,)),
        ],
        cost_estimate=pl.CostEstimate(
            flops=2 * devices * CAP * members * count * width, bytes_accessed=4 * MIB, transcendentals=0
        ),
        compiler_params=pltpu.CompilerParams(vmem_limit_bytes=63 * MIB),
        name="pack",
    )(ident, weight, rows)


def hot_kernel(place_ref, hot_ref):
    count, total = hot_ref.shape
    for row, first, last in ((0, 0, total - total // 5), (1, total - total // 5, total)):
        place = column_of(place_ref[row : row + 1, :])
        for start in range(first, last, LANES):
            hot = place == start - first + iota((count, LANES), 1)
            hot_ref[:, start : start + LANES] = hot.astype(BF16)


def hot_rows(place, devices, members):
    count = place.shape[1]
    total = devices * CAP * (members + 1)
    return pl.pallas_call(
        hot_kernel,
        out_shape=jax.ShapeDtypeStruct((count, total), BF16),
        in_specs=[IN_VMEM],
        out_specs=IN_VMEM,
        cost_estimate=pl.CostEstimate(flops=count * total, bytes_accessed=MIB, transcendentals=0),
        compiler_params=pltpu.CompilerParams(vmem_limit_bytes=8 * MIB),
        name="hot_rows",
    )(place)


def cluster_kernel(sharp_ref, got_ref, back_hbm, rows_s, prob_s, done_s, back_s, sems):
    members = sharp_ref.shape[1]
    devices, cap, wide = got_ref.shape
    width = (wide - LANES) // members
    each = devices * cap
    diagonal = iota((each, each), 0) == iota((each, each), 1)
    lane = iota((each, LANES), 1)
    weights = turned(got_ref[:, :, members * width :].reshape(each, LANES).astype(F32))
    scores = jnp.zeros((each, LANES), F32)
    copies = []
    grams, inverses = {}, {}

    def take(member):
        rows_s[member] = got_ref[:, :, member * width : (member + 1) * width].reshape(each, width)

    def products(member):
        grams[member] = dot(rows_s[member], rows_s[member], ((1,), (1,)))

    def weigh(member, scores):
        gram = grams[member]
        sharp = sharp_ref[0, member]
        rate = sharp * LOG2_E
        squares = jnp.where(diagonal, gram, F32(0.0))
        by_row = lax.rsqrt(jnp.sum(squares, axis=1, keepdims=True) + 1e-06) * rate
        by_col = lax.rsqrt(jnp.sum(squares, axis=0, keepdims=True) + 1e-06)
        scaled = jnp.where(diagonal, F32(0.0), gram * by_col * by_row)
        expo = weights[member : member + 1, :] * jnp.exp2(scaled - rate)
        total = jnp.sum(expo, axis=1, keepdims=True)
        prob_s[member] = expo.astype(BF16)
        inverses[member] = 1.0 / total
        return jnp.where(lane == member, jnp.log(total) + sharp, scores)

    def smooth(member, index):
        of = slice(index * BLOCK, (index + 1) * BLOCK)
        numer = dot(prob_s[member], rows_s[member, :, of])
        done_s[member, :, of] = (numer * inverses[member]).astype(BF16)

    def give(member, last):
        first = member * width
        back_s[:, :, first : first + width] = done_s[member].reshape(devices, cap, width)
        copies.append(
            pltpu.make_async_copy(
                back_s.at[:, :, first:last], back_hbm.at[:, :, first:last], sems.at[member]
            )
        )
        copies[-1].start()

    pairs = [tuple(range(at, min(at + 2, members))) for at in range(0, members, 2)]
    for turn in range(len(pairs) + 2):
        if turn < len(pairs):
            for member in pairs[turn]:
                take(member)
            for member in pairs[turn]:
                products(member)
        if 1 <= turn <= len(pairs):
            for index in range(width // BLOCK):
                for member in pairs[turn - 1]:
                    smooth(member, index)
        if turn < len(pairs):
            for member in pairs[turn]:
                scores = weigh(member, scores)
        if turn == len(pairs) - 1:
            back_s[:, :, members * width :] = scores.astype(BF16).reshape(devices, cap, LANES)
        if 1 <= turn <= len(pairs):
            for member in pairs[turn - 1]:
                give(member, wide if member == members - 1 else (member + 1) * width)
    for copy in copies:
        copy.wait()


def clusters(sharp, got):
    members = sharp.shape[1]
    devices, cap, wide = got.shape
    width = (wide - LANES) // members
    return pl.pallas_call(
        cluster_kernel,
        out_shape=pltpu.HBM(got.shape, BF16),
        in_specs=[IN_SMEM, IN_VMEM],
        out_specs=IN_HBM,
        scratch_shapes=[
            pltpu.VMEM((members, devices * cap, width), BF16),
            pltpu.VMEM((members, devices * cap, devices * cap), BF16),
            pltpu.VMEM((members, devices * cap, width), BF16),
            pltpu.VMEM(got.shape, BF16),
            pltpu.SemaphoreType.DMA((members,)),
        ],
        compiler_params=pltpu.CompilerParams(vmem_limit_bytes=20 * MIB),
        name="clusters",
    )(sharp, got)


def home_kernel(members, hot_ref, place_ref, home_ref, smooth_hbm, score_ref, rows_s, smooth_s, sems):
    blocks, count, block = smooth_s.shape
    devices, cap, wide = home_ref.shape
    width = blocks * block
    each = devices * cap
    copies = []
    for m in range(members):
        rows = home_ref[:, :, m * width : (m + 1) * width].reshape(each, width)
        rows_s[m * each : (m + 1) * each, :] = rows
    for index in range(blocks):
        rows = rows_s[:, index * block : (index + 1) * block]
        smooth_s[index] = dot(hot_ref[:, 0 : members * each], rows).astype(BF16)
        of = slice(index * block, (index + 1) * block)
        copies.append(pltpu.make_async_copy(smooth_s.at[index], smooth_hbm.at[:, of], sems.at[index]))
        copies[-1].start()
    scores = home_ref[:, :, members * width :].reshape(each, LANES)
    taken = turned(dot(hot_ref[:, members * each :], scores))
    own_lane = iota((LANES, count), 0) == place_ref[2:3, :]
    score = jnp.sum(jnp.where(own_lane, taken, F32(0.0)), axis=0, keepdims=True)
    score_ref[...] = score.astype(BF16).reshape(score_ref.shape)
    for copy in copies:
        copy.wait()


def bring_home(hot, place, home, members):
    count = hot.shape[0]
    width = (home.shape[2] - LANES) // members

    def kernel(*refs):
        home_kernel(members, *refs)

    return pl.pallas_call(
        kernel,
        out_shape=(jax.ShapeDtypeStruct((count, width), BF16), jax.ShapeDtypeStruct((count,), BF16)),
        in_specs=[IN_VMEM] * 3,
        out_specs=(IN_HBM, IN_VMEM),
        scratch_shapes=[
            pltpu.VMEM((home.shape[0] * home.shape[1] * members, width), BF16),
            pltpu.VMEM((width // BLOCK, count, BLOCK), BF16),
            pltpu.SemaphoreType.DMA((width // BLOCK,)),
        ],
        compiler_params=pltpu.CompilerParams(vmem_limit_bytes=16 * MIB),
        name="bring_home",
    )(hot, place, home)


def local(sentence_vectors, group_assignment, adjacent_importance, group_sharpness):
    devices = lax.axis_size("own")
    members = group_sharpness.shape[0]
    row_count = sentence_vectors.shape[0]
    send, place = pack(
        group_assignment.reshape(1, row_count), adjacent_importance, sentence_vectors, devices, members
    )
    got = lax.all_to_all(send, "own", split_axis=0, concat_axis=0, tiled=True)
    sharp = group_sharpness.astype(F32).reshape(1, members)
    back = clusters(sharp, got)
    hot = hot_rows(place, devices, members)
    home = lax.all_to_all(back, "own", split_axis=0, concat_axis=0, tiled=True)
    return bring_home(hot, place, home, members)


def solution(mesh):
    placed = (P("own", None), P("own", None), P("own"), P("own"))
    return jax.shard_map(
        local, mesh=mesh, in_specs=placed, out_specs=(P("own", None), P("own")), check_vma=False
    )
```

time: 97 us -> 89.4 us (0.922)
  local copies, waits for them, and re-layouts: 5.41 us -> 0.01 us
  waiting for transfers between devices: 65.7 us -> 61.4 us
  Pallas kernels: 8.09 us -> 10.7 us
    unnamed x10 -> x4, local copies, waits for them, and re-layouts: 4.73 us -> 0.01 us
    pallas_call x4, Pallas kernels: 8.09 us -> 10.7 us  [the longest x1 3.87 us: clusters(): pl.pallas_call(cluster_kernel, out_shape=pltpu.HBM(got.shape, BF16), in_s...]
    all_to_all x1, waiting for transfers between devices: 32.8 us -> 30.6 us  [local(): home = lax.all_to_all(back, 'own', split_axis=0, concat_axis=0, tiled=True)]
    all_to_all x1, waiting for transfers between devices: 32.9 us -> 30.8 us  [local(): got = lax.all_to_all(send, 'own', split_axis=0, concat_axis=0, tiled=True)]
where the time goes in v2:
time: 89.4 us; the launch traced here: 89.1 us
  waiting for transfers between devices  61.4 us (69%)
  starting transfers between devices  16.2 us (18%)
  Pallas kernels  10.7 us (12%)
    all_to_all x1, waiting for transfers between devices, local(): got = lax.all_to_all(send, 'own', split_axis=0, concat_axis=0, tiled=True)  30.8 us
    all_to_all x1, waiting for transfers between devices, local(): home = lax.all_to_all(back, 'own', split_axis=0, concat_axis=0, tiled=True)  30.6 us
    all_to_all x1, starting transfers between devices, local(): got = lax.all_to_all(send, 'own', split_axis=0, concat_axis=0, tiled=True)  11.5 us
    all_to_all x1, starting transfers between devices, local(): home = lax.all_to_all(back, 'own', split_axis=0, concat_axis=0, tiled=True)  4.74 us
    pallas_call x1, Pallas kernels, clusters(): pl.pallas_call(cluster_kernel, out_shape=pltpu.HBM(got.shape, BF16), in_s...  3.87 us
    pallas_call x1, Pallas kernels, pack(): pl.pallas_call(kernel, out_shape=(pltpu.HBM((devices, CAP, wide), BF16),...  3.56 us
    pallas_call x1, Pallas kernels, bring_home(): pl.pallas_call(kernel, out_shape=(jax.ShapeDtypeStruct((count, width), BF...  2.95 us
  transfers between devices with their start and end apart: 2, of which 2 were waited for; matrix products, arithmetic and copies ran while one was open for 0% of the time, Pallas kernels for 0%

profile of v2, /device:TPU:1, one launch (start us, length us, event | category | flops | bytes accessed | tf_op | source)
XLA Modules:
  0.0 89.1 jit_solution(12313290451880483731)
XLA Ops:
  0.6 3.6 %pack.1 = (bf16[128,2,4224]{2,1,0:T(2,128)(2,1)}, s32[3,512]{1,0:T(4,128)}) custom-call(s32[1,512]{1,0:T(1,128)} %bitcast.4, bf16[512]{0:T(512)(128)(2,1)} %refs_1_.1, bf16[512,1024]{1,0:T(8,128)(2,1)} %refs_2_.1), custom_call_target="tpu_custom_call" | custom-call | flops 1073741824 | bytes 4194304 | tf_op jit(solution)/shard_map/pack/pallas_call | solution.py:117
  4.2 0.0 copy-start.1
  4.2 11.5 %all-to-all-start = ((bf16[128,2,4224]{2,1,0:T(2,128)(2,1)}), bf16[128,2,4224]{2,1,0:T(2,128)(2,1)S(1)}, u32[]{:S(2)}, u32[]{:S(2)}) async-start(bf16[128,2,4224]{2,1,0:T(2,128)(2,1)} %get-tuple-element.5), calls=%async_computation | async-start | bytes 4325376 | tf_op jit(solution)/shard_map/all_to_all | solution.py:308
  15.7 0.0 copy-done.1
  15.7 30.8 %all-to-all-done.got_ref = bf16[128,2,4224]{2,1,0:T(2,128)(2,1)S(1)} async-done(((bf16[128,2,4224]{2,1,0:T(2,128)(2,1)}), bf16[128,2,4224]{2,1,0:T(2,128)(2,1)S(1)}, u32[]{:S(2)}, u32[]{:S(2)}) %all-to-all-start) | async-done | bytes 2162720 | tf_op jit(solution)/shard_map/all_to_all | solution.py:308
  46.5 3.9 %clusters.1 = bf16[128,2,4224]{2,1,0:T(2,128)(2,1)} custom-call(f32[1,4]{1,0:T(1,128)S(1)} %bitcast_convert_fusion.sharp_ref, bf16[128,2,4224]{2,1,0:T(2,128)(2,1)S(1)} %all-to-all-done.got_ref), custom_call_target="tpu_custom_call" | custom-call | tf_op jit(solution)/shard_map/clusters/pallas_call | solution.py:238
  50.4 0.0 copy-start
  50.4 4.7 %all-to-all-start.1 = ((bf16[128,2,4224]{2,1,0:T(2,128)(2,1)}), bf16[128,2,4224]{2,1,0:T(2,128)(2,1)S(1)}, u32[]{:S(2)}, u32[]{:S(2)}) async-start(bf16[128,2,4224]{2,1,0:T(2,128)(2,1)} %clusters.1), calls=%async_computation.1 | async-start | bytes 4325376 | tf_op jit(solution)/shard_map/all_to_all | solution.py:312
  55.2 0.0 copy-done
  55.2 0.3 hot_rows.1.refs_0_
  55.5 30.6 %all-to-all-done.1.refs_2_ = bf16[128,2,4224]{2,1,0:T(2,128)(2,1)S(1)} async-done(((bf16[128,2,4224]{2,1,0:T(2,128)(2,1)}), bf16[128,2,4224]{2,1,0:T(2,128)(2,1)S(1)}, u32[]{:S(2)}, u32[]{:S(2)}) %all-to-all-start.1) | async-done | bytes 2162720 | tf_op jit(solution)/shard_map/all_to_all | solution.py:312
  86.1 2.9 %bring_home.1 = (bf16[512,1024]{1,0:T(8,128)(2,1)}, bf16[512]{0:T(512)(128)(2,1)}) custom-call(bf16[512,1280]{1,0:T(8,128)(2,1)S(1)} %hot_rows.1.refs_0_, s32[3,512]{1,0:T(4,128)S(1)} %copy-done, bf16[128,2,4224]{2,1,0:T(2,128)(2,1)S(1)} %all-to-all-done.1.refs_2_), custom_call_target="tpu_custom_call" | custom-call | tf_op jit(solution)/shard_map/bring_home/pallas_call | solution.py:286
  (1 shorter events, 0.0 us)
Async XLA Ops:
  4.2 11.5 %copy-start.1 = (bf16[4]{0:T(256)(128)(2,1)S(1)}, bf16[4]{0:T(256)(128)(2,1)}, u32[]{:S(2)}) copy-start(bf16[4]{0:T(256)(128)(2,1)} %param.7) | copy-start | bytes 28
  4.2 42.3 %all-to-all-start = ((bf16[128,2,4224]{2,1,0:T(2,128)(2,1)}), bf16[128,2,4224]{2,1,0:T(2,128)(2,1)S(1)}, u32[]{:S(2)}, u32[]{:S(2)}) async-start(bf16[128,2,4224]{2,1,0:T(2,128)(2,1)} %get-tuple-element.5), calls=%async_computation | async-start | bytes 4325376 | tf_op jit(solution)/shard_map/all_to_all | solution.py:308
  50.4 4.8 %copy-start = (s32[3,512]{1,0:T(4,128)S(1)}, s32[3,512]{1,0:T(4,128)}, u32[]{:S(2)}) copy-start(s32[3,512]{1,0:T(4,128)} %get-tuple-element.4.place_ref.refs_1_) | copy-start | bytes 18436
  50.4 35.7 %all-to-all-start.1 = ((bf16[128,2,4224]{2,1,0:T(2,128)(2,1)}), bf16[128,2,4224]{2,1,0:T(2,128)(2,1)S(1)}, u32[]{:S(2)}, u32[]{:S(2)}) async-start(bf16[128,2,4224]{2,1,0:T(2,128)(2,1)} %clusters.1), calls=%async_computation.1 | async-start | bytes 4325376 | tf_op jit(solution)/shard_map/all_to_all | solution.py:312

commit v3 on v2

--- a/solution.py
+++ b/solution.py
@@ -10,11 +10,12 @@
 LANES = 128
 CAP = 2
 BLOCK = 256
+HALVES = 2
 PARTS = 2
+CHUNK = 64
 LOG2_E = 1.4426950408889634
 MIB = 1 << 20
 IN_VMEM = pl.BlockSpec(memory_space=pltpu.VMEM)
-IN_SMEM = pl.BlockSpec(memory_space=pltpu.SMEM)
 IN_HBM = pl.BlockSpec(memory_space=pltpu.HBM)
 
 
@@ -39,6 +40,12 @@
     for start in range(0, tall.shape[0], LANES):
         parts.append(jnp.transpose(tall[start : start + LANES, :]))
     return jnp.concatenate(parts, axis=1)
+
+
+def hot_of(row, each):
+    spread = iota((each, row.shape[1]), 0).astype(F32).astype(BF16)
+    hit = row.astype(F32).astype(BF16) == spread
+    return jnp.where(hit, BF16(1.0), BF16(0.0))
 
 
 def pack_kernel(
@@ -62,9 +69,13 @@
     ranks = []
     for start in range(0, count, LANES):
         here = ident[:, start : start + LANES]
-        same = ident_col == here
-        earlier = iota((count, LANES), 0) < iota((count, LANES), 1) + start
-        ranks.append(jnp.sum((same & earlier).astype(jnp.int32), axis=0, keepdims=True))
+        same = ident_col[start : start + LANES, :] == here
+        earlier = iota((LANES, LANES), 0) < iota((LANES, LANES), 1)
+        rank = jnp.sum((same & earlier).astype(jnp.int32), axis=0, keepdims=True)
+        if start > 0:
+            before = ident_col[0:start, :] == here
+            rank = rank + jnp.sum(before.astype(jnp.int32), axis=0, keepdims=True)
+        ranks.append(rank)
     member = ident % members
     within = ident // members * CAP + jnp.concatenate(ranks, axis=1)
     place = member * each + within
@@ -74,19 +85,21 @@
     put_place = pltpu.make_async_copy(place_s, place_hbm, sems.at[2])
     put_place.start()
     get_weight.wait()
-    weight = weight_s[...].astype(F32).reshape(1, count)
-    own_lane = iota((LANES, count), 0) == member
-    weights = turned_back(jnp.where(own_lane, weight, F32(0.0))).astype(BF16)
-    hot = (within == iota((each, count), 0)).astype(BF16)
-    send_s[:, :, members * width :] = dot(hot, weights).astype(BF16).reshape(devices, CAP, LANES)
     for copy in get_rows:
         copy.wait()
     copies = []
     for index in range(members):
-        hot = (place == index * each + iota((each, count), 0)).astype(BF16)
+        hot = hot_of(jnp.where(member == index, within, -1), each)
         packed = dot(hot, rows_s[...]).astype(BF16)
         first, last = index * width, (index + 1) * width
         send_s[:, :, first:last] = packed.reshape(devices, CAP, width)
+        if index == 0:
+            weight = weight_s[...].astype(F32).reshape(1, count)
+            own_lane = iota((LANES, count), 0) == member
+            weights = turned_back(jnp.where(own_lane, weight, F32(0.0))).astype(BF16)
+            hot = hot_of(within, each)
+            weights = dot(hot, weights).astype(BF16).reshape(devices, CAP, LANES)
+            send_s[:, :, members * width :] = weights
         if index == members - 1:
             last = last + LANES
         copies.append(
@@ -161,8 +174,8 @@
     )(place)
 
 
-def cluster_kernel(sharp_ref, got_ref, back_hbm, rows_s, prob_s, done_s, back_s, sems):
-    members = sharp_ref.shape[1]
+def cluster_kernel(sharp_ref, got_ref, back_hbm, rows_s, unit_s, prob_s, done_s, back_s, sems):
+    members = sharp_ref.shape[0]
     devices, cap, wide = got_ref.shape
     width = (wide - LANES) // members
     each = devices * cap
@@ -176,22 +189,27 @@
     def take(member):
         rows_s[member] = got_ref[:, :, member * width : (member + 1) * width].reshape(each, width)
 
+
+    def norms(member):
+        for start in range(0, each, CHUNK):
+            wider = rows_s[member, start : start + CHUNK, :].astype(F32)
+            square_sum = jnp.sum(wider * wider, axis=1, keepdims=True)
+            unit = wider * lax.rsqrt(square_sum + 1e-06)
+            unit_s[member, start : start + CHUNK, :] = unit.astype(BF16)
+
     def products(member):
-        grams[member] = dot(rows_s[member], rows_s[member], ((1,), (1,)))
+        grams[member] = dot(unit_s[member], unit_s[member], ((1,), (1,)))
 
     def weigh(member, scores):
         gram = grams[member]
-        sharp = sharp_ref[0, member]
+        sharp = sharp_ref[member : member + 1, :]
         rate = sharp * LOG2_E
-        squares = jnp.where(diagonal, gram, F32(0.0))
-        by_row = lax.rsqrt(jnp.sum(squares, axis=1, keepdims=True) + 1e-06) * rate
-        by_col = lax.rsqrt(jnp.sum(squares, axis=0, keepdims=True) + 1e-06)
-        scaled = jnp.where(diagonal, F32(0.0), gram * by_col * by_row)
-        expo = weights[member : member + 1, :] * jnp.exp2(scaled - rate)
+        cosine = jnp.where(diagonal, F32(0.0), gram)
+        expo = weights[member : member + 1, :] * jnp.exp2(rate * cosine - rate)
         total = jnp.sum(expo, axis=1, keepdims=True)
         prob_s[member] = expo.astype(BF16)
         inverses[member] = 1.0 / total
-        return jnp.where(lane == member, jnp.log(total) + sharp, scores)
+        return jnp.where(lane == member, jnp.log(total) + sharp[:, 0:LANES], scores)
 
     def smooth(member, index):
         of = slice(index * BLOCK, (index + 1) * BLOCK)
@@ -209,16 +227,17 @@
         copies[-1].start()
 
     pairs = [tuple(range(at, min(at + 2, members))) for at in range(0, members, 2)]
+    for member in pairs[0]:
+        take(member)
+        norms(member)
     for turn in range(len(pairs) + 2):
         if turn < len(pairs):
             for member in pairs[turn]:
+                products(member)
+        if turn + 1 < len(pairs):
+            for member in pairs[turn + 1]:
                 take(member)
-            for member in pairs[turn]:
-                products(member)
-        if 1 <= turn <= len(pairs):
-            for index in range(width // BLOCK):
-                for member in pairs[turn - 1]:
-                    smooth(member, index)
+                norms(member)
         if turn < len(pairs):
             for member in pairs[turn]:
                 scores = weigh(member, scores)
@@ -226,21 +245,24 @@
             back_s[:, :, members * width :] = scores.astype(BF16).reshape(devices, cap, LANES)
         if 1 <= turn <= len(pairs):
             for member in pairs[turn - 1]:
+                for index in range(width // BLOCK):
+                    smooth(member, index)
                 give(member, wide if member == members - 1 else (member + 1) * width)
     for copy in copies:
         copy.wait()
 
 
 def clusters(sharp, got):
-    members = sharp.shape[1]
+    members = sharp.shape[0]
     devices, cap, wide = got.shape
     width = (wide - LANES) // members
     return pl.pallas_call(
         cluster_kernel,
         out_shape=pltpu.HBM(got.shape, BF16),
-        in_specs=[IN_SMEM, IN_VMEM],
+        in_specs=[IN_VMEM] * 2,
         out_specs=IN_HBM,
         scratch_shapes=[
+            pltpu.VMEM((members, devices * cap, width), BF16),
             pltpu.VMEM((members, devices * cap, width), BF16),
             pltpu.VMEM((members, devices * cap, devices * cap), BF16),
             pltpu.VMEM((members, devices * cap, width), BF16),
@@ -252,26 +274,26 @@
     )(sharp, got)
 
 
-def home_kernel(members, hot_ref, place_ref, home_ref, smooth_hbm, score_ref, rows_s, smooth_s, sems):
-    blocks, count, block = smooth_s.shape
+def home_kernel(members, hot_ref, place_ref, home_ref, smooth_hbm, score_hbm, rows_s, smooth_s, score_s, sems):
+    count, width = smooth_s.shape
     devices, cap, wide = home_ref.shape
-    width = blocks * block
+    blocks = 2
     each = devices * cap
-    copies = []
+    scores = home_ref[:, :, members * width :].reshape(each, LANES)
+    taken = turned(dot(hot_ref[:, members * each :], scores))
+    own_lane = iota((LANES, count), 0) == place_ref[2:3, :]
+    score = jnp.sum(jnp.where(own_lane, taken, F32(0.0)), axis=0, keepdims=True)
+    score_s[...] = score.astype(BF16).reshape(score_s.shape)
+    copies = [pltpu.make_async_copy(score_s, score_hbm, sems.at[blocks])]
+    copies[0].start()
     for m in range(members):
         rows = home_ref[:, :, m * width : (m + 1) * width].reshape(each, width)
         rows_s[m * each : (m + 1) * each, :] = rows
     for index in range(blocks):
-        rows = rows_s[:, index * block : (index + 1) * block]
-        smooth_s[index] = dot(hot_ref[:, 0 : members * each], rows).astype(BF16)
-        of = slice(index * block, (index + 1) * block)
-        copies.append(pltpu.make_async_copy(smooth_s.at[index], smooth_hbm.at[:, of], sems.at[index]))
+        of = slice(index * count // blocks, (index + 1) * count // blocks)
+        smooth_s[of, :] = dot(hot_ref[of, 0 : members * each], rows_s[...]).astype(BF16)
+        copies.append(pltpu.make_async_copy(smooth_s.at[of, :], smooth_hbm.at[of, :], sems.at[index]))
         copies[-1].start()
-    scores = home_ref[:, :, members * width :].reshape(each, LANES)
-    taken = turned(dot(hot_ref[:, members * each :], scores))
-    own_lane = iota((LANES, count), 0) == place_ref[2:3, :]
-    score = jnp.sum(jnp.where(own_lane, taken, F32(0.0)), axis=0, keepdims=True)
-    score_ref[...] = score.astype(BF16).reshape(score_ref.shape)
     for copy in copies:
         copy.wait()
 
@@ -287,11 +309,12 @@
         kernel,
         out_shape=(jax.ShapeDtypeStruct((count, width), BF16), jax.ShapeDtypeStruct((count,), BF16)),
         in_specs=[IN_VMEM] * 3,
-        out_specs=(IN_HBM, IN_VMEM),
+        out_specs=(IN_HBM, IN_HBM),
         scratch_shapes=[
             pltpu.VMEM((home.shape[0] * home.shape[1] * members, width), BF16),
-            pltpu.VMEM((width // BLOCK, count, BLOCK), BF16),
-            pltpu.SemaphoreType.DMA((width // BLOCK,)),
+            pltpu.VMEM((count, width), BF16),
+            pltpu.VMEM((count,), BF16),
+            pltpu.SemaphoreType.DMA((HALVES + 1,)),
         ],
         compiler_params=pltpu.CompilerParams(vmem_limit_bytes=16 * MIB),
         name="bring_home",
@@ -306,7 +329,7 @@
         group_assignment.reshape(1, row_count), adjacent_importance, sentence_vectors, devices, members
     )
     got = lax.all_to_all(send, "own", split_axis=0, concat_axis=0, tiled=True)
-    sharp = group_sharpness.astype(F32).reshape(1, members)
+    sharp = jnp.broadcast_to(group_sharpness.astype(F32)[:, None], (members, devices * CAP))
     back = clusters(sharp, got)
     hot = hot_rows(place, devices, members)
     home = lax.all_to_all(back, "own", split_axis=0, concat_axis=0, tiled=True)

time: 89.4 us -> 88.4 us (0.989)
  blocking collectives: 0 us -> 42.3 us
  waiting for transfers between devices: 61.4 us -> 30.6 us
  starting transfers between devices: 16.2 us -> 4.74 us
  Pallas kernels: 10.7 us -> 9.68 us
    all_to_all x0 -> x1, blocking collectives: none -> 42.3 us  [local(): got = lax.all_to_all(send, 'own', split_axis=0, concat_axis=0, tiled=True)]
    all_to_all x1 -> x0, waiting for transfers between devices: 30.8 us -> none  [local(): got = lax.all_to_all(send, 'own', split_axis=0, concat_axis=0, tiled=True)]
    all_to_all x1 -> x0, starting transfers between devices: 11.5 us -> none  [local(): got = lax.all_to_all(send, 'own', split_axis=0, concat_axis=0, tiled=True)]
  transfers between devices with their start and end apart: 2 -> 1, of which waited for: 2 -> 1; matrix products, arithmetic and copies ran while one was open for 0% -> 0% of each run, Pallas kernels for 0% -> 0%
where the time goes in v3:
time: 88.4 us; the launch traced here: 88.1 us
  blocking collectives  42.3 us (48%)
  waiting for transfers between devices  30.6 us (35%)
  Pallas kernels  9.68 us (11%)
  starting transfers between devices  4.74 us (5%)
    all_to_all x1, blocking collectives, local(): got = lax.all_to_all(send, 'own', split_axis=0, concat_axis=0, tiled=True)  42.3 us
    all_to_all x1, waiting for transfers between devices, local(): home = lax.all_to_all(back, 'own', split_axis=0, concat_axis=0, tiled=True)  30.6 us
    all_to_all x1, starting transfers between devices, local(): home = lax.all_to_all(back, 'own', split_axis=0, concat_axis=0, tiled=True)  4.74 us
    pallas_call x1, Pallas kernels, pack(): pl.pallas_call(kernel, out_shape=(pltpu.HBM((devices, CAP, wide), BF16),...  3.6 us
    pallas_call x1, Pallas kernels, clusters(): pl.pallas_call(cluster_kernel, out_shape=pltpu.HBM(got.shape, BF16), in_s...  3.43 us
    pallas_call x1, Pallas kernels, bring_home(): pl.pallas_call(kernel, out_shape=(jax.ShapeDtypeStruct((count, width), BF...  2.33 us
  transfers between devices with their start and end apart: 1, of which 1 were waited for; matrix products, arithmetic and copies ran while one was open for 0% of the time, Pallas kernels for 0%

profile of v3, /device:TPU:1, one launch (start us, length us, event | category | flops | bytes accessed | tf_op | source)
XLA Modules:
  0.0 88.1 jit_solution(17195338502284396125)
XLA Ops:
  0.6 3.6 %pack.1 = (bf16[128,2,4224]{2,1,0:T(2,128)(2,1)}, s32[3,512]{1,0:T(4,128)}) custom-call(s32[1,512]{1,0:T(1,128)} %bitcast.1, bf16[512]{0:T(512)(128)(2,1)} %refs_1_.1, bf16[512,1024]{1,0:T(8,128)(2,1)} %refs_2_.1), custom_call_target="tpu_custom_call" | custom-call | flops 1073741824 | bytes 4194304 | tf_op jit(solution)/shard_map/pack/pallas_call | solution.py:130
  4.2 0.0 copy-start.1
  4.2 42.3 %all_to_all.10.got_ref = bf16[128,2,4224]{2,1,0:T(2,128)(2,1)S(1)} all-to-all(bf16[128,2,4224]{2,1,0:T(2,128)(2,1)} %get-tuple-element.5), channel_id=1, replica_groups=mesh['own'=128] {'own'}, dimensions={0} | all-to-all | bytes 4325376 | tf_op jit(solution)/shard_map/all_to_all | solution.py:331
  46.6 0.0 copy-done.1
  46.6 0.1 broadcast_in_dim.2.sharp_ref
  46.6 3.4 %clusters.1 = bf16[128,2,4224]{2,1,0:T(2,128)(2,1)} custom-call(f32[4,256]{1,0:T(4,128)S(1)} %broadcast_in_dim.2.sharp_ref, bf16[128,2,4224]{2,1,0:T(2,128)(2,1)S(1)} %all_to_all.10.got_ref), custom_call_target="tpu_custom_call" | custom-call | tf_op jit(solution)/shard_map/clusters/pallas_call | solution.py:259
  50.1 0.0 copy-start
  50.1 4.7 %all-to-all-start.1 = ((bf16[128,2,4224]{2,1,0:T(2,128)(2,1)}), bf16[128,2,4224]{2,1,0:T(2,128)(2,1)S(1)}, u32[]{:S(2)}, u32[]{:S(2)}) async-start(bf16[128,2,4224]{2,1,0:T(2,128)(2,1)} %clusters.1), calls=%async_computation.1 | async-start | bytes 4325376 | tf_op jit(solution)/shard_map/all_to_all | solution.py:335
  54.8 0.0 copy-done
  54.8 0.3 hot_rows.1.refs_0_
  55.2 30.6 %all-to-all-done.1.refs_2_ = bf16[128,2,4224]{2,1,0:T(2,128)(2,1)S(1)} async-done(((bf16[128,2,4224]{2,1,0:T(2,128)(2,1)}), bf16[128,2,4224]{2,1,0:T(2,128)(2,1)S(1)}, u32[]{:S(2)}, u32[]{:S(2)}) %all-to-all-start.1) | async-done | bytes 2162720 | tf_op jit(solution)/shard_map/all_to_all | solution.py:335
  85.8 2.3 %bring_home.1 = (bf16[512,1024]{1,0:T(8,128)(2,1)}, bf16[512]{0:T(512)(128)(2,1)}) custom-call(bf16[512,1280]{1,0:T(8,128)(2,1)S(1)} %hot_rows.1.refs_0_, s32[3,512]{1,0:T(4,128)S(1)} %copy-done, bf16[128,2,4224]{2,1,0:T(2,128)(2,1)S(1)} %all-to-all-done.1.refs_2_), custom_call_target="tpu_custom_call" | custom-call | tf_op jit(solution)/shard_map/bring_home/pallas_call | solution.py:308
Async XLA Ops:
  4.2 42.3 %copy-start.1 = (bf16[4]{0:T(256)(128)(2,1)S(1)}, bf16[4]{0:T(256)(128)(2,1)}, u32[]{:S(2)}) copy-start(bf16[4]{0:T(256)(128)(2,1)} %param.7) | copy-start | bytes 28
  50.1 4.8 %copy-start = (s32[3,512]{1,0:T(4,128)S(1)}, s32[3,512]{1,0:T(4,128)}, u32[]{:S(2)}) copy-start(s32[3,512]{1,0:T(4,128)} %get-tuple-element.4.place_ref.refs_1_) | copy-start | bytes 18436
  50.1 35.7 %all-to-all-start.1 = ((bf16[128,2,4224]{2,1,0:T(2,128)(2,1)}), bf16[128,2,4224]{2,1,0:T(2,128)(2,1)S(1)}, u32[]{:S(2)}, u32[]{:S(2)}) async-start(bf16[128,2,4224]{2,1,0:T(2,128)(2,1)} %clusters.1), calls=%async_computation.1 | async-start | bytes 4325376 | tf_op jit(solution)/shard_map/all_to_all | solution.py:335

commit v4 on v3

--- a/solution.py
+++ b/solution.py
@@ -96,10 +96,14 @@
         if index == 0:
             weight = weight_s[...].astype(F32).reshape(1, count)
             own_lane = iota((LANES, count), 0) == member
-            weights = turned_back(jnp.where(own_lane, weight, F32(0.0))).astype(BF16)
-            hot = hot_of(within, each)
-            weights = dot(hot, weights).astype(BF16).reshape(devices, CAP, LANES)
-            send_s[:, :, members * width :] = weights
+            ones = iota((LANES, count), 0) == members
+            mixed = jnp.where(own_lane, weight, jnp.where(ones, F32(1.0), F32(0.0)))
+            tile = dot(hot_of(within, each), turned_back(mixed).astype(BF16))
+            lane, second = iota((each, LANES), 1), iota((each, LANES), 0) % CAP == 1
+            counts = jnp.where((lane == members) & second, tile, F32(0.0))
+            most = jnp.max(jnp.max(counts, axis=1, keepdims=True), axis=0, keepdims=True)
+            tile = jnp.where(lane == members, most, tile)
+            send_s[:, :, members * width :] = tile.astype(BF16).reshape(devices, CAP, LANES)
         if index == members - 1:
             last = last + LANES
         copies.append(
@@ -151,133 +155,215 @@
     )(ident, weight, rows)
 
 
-def hot_kernel(place_ref, hot_ref):
-    count, total = hot_ref.shape
-    for row, first, last in ((0, 0, total - total // 5), (1, total - total // 5, total)):
-        place = column_of(place_ref[row : row + 1, :])
-        for start in range(first, last, LANES):
-            hot = place == start - first + iota((count, LANES), 1)
-            hot_ref[:, start : start + LANES] = hot.astype(BF16)
+def hot_kernel(each, members, place_ref, full_ref, short_ref):
+    count = full_ref.shape[0]
+    place, within, member = place_ref[0:1, :], place_ref[1:2, :], place_ref[2:3, :]
+    owner, rank = within // CAP, within % CAP
+    key = jnp.where(rank == 1, owner * members + member, -members)
+    key_col = column_of(key)
+    extras = []
+    for start in range(0, count, LANES):
+        here = key[:, start : start + LANES]
+        fewer = (key_col < here) & (key_col >= here - here % members)
+        extras.append(jnp.sum(fewer.astype(jnp.int32), axis=0, keepdims=True))
+    extra = jnp.concatenate(extras, axis=1)
+    first = member // CAP * each + owner * CAP + member % CAP
+    short = jnp.where(rank == 1, members // CAP * each + owner * CAP + extra, first)
+    for ref, where in ((full_ref, place), (short_ref, short)):
+        total = ref.shape[1] - each
+        for low, high, row in ((0, total, where), (total, total + each, within)):
+            spot = column_of(row)
+            for start in range(low, high, LANES):
+                hot = spot == start - low + iota((count, LANES), 1)
+                ref[:, start : start + LANES] = hot.astype(BF16)
 
 
 def hot_rows(place, devices, members):
     count = place.shape[1]
-    total = devices * CAP * (members + 1)
+    each = devices * CAP
+    shapes = [(count, each * (blocks + 1)) for blocks in (members, members // CAP + 1)]
+
+    def kernel(*refs):
+        hot_kernel(each, members, *refs)
+
     return pl.pallas_call(
-        hot_kernel,
-        out_shape=jax.ShapeDtypeStruct((count, total), BF16),
+        kernel,
+        out_shape=[jax.ShapeDtypeStruct(shape, BF16) for shape in shapes],
         in_specs=[IN_VMEM],
-        out_specs=IN_VMEM,
-        cost_estimate=pl.CostEstimate(flops=count * total, bytes_accessed=MIB, transcendentals=0),
+        out_specs=[IN_VMEM] * 2,
+        cost_estimate=pl.CostEstimate(
+            flops=2 * count * each * members, bytes_accessed=2 * MIB, transcendentals=0
+        ),
         compiler_params=pltpu.CompilerParams(vmem_limit_bytes=8 * MIB),
         name="hot_rows",
     )(place)
 
 
-def cluster_kernel(sharp_ref, got_ref, back_hbm, rows_s, unit_s, prob_s, done_s, back_s, sems):
+def cluster_kernel(
+    sharp_ref, got_ref, short_hbm, full_hbm, most_ref, rows_s, unit_s, prob_s, left_s, done_s, sent_s, sems
+):
     members = sharp_ref.shape[0]
     devices, cap, wide = got_ref.shape
     width = (wide - LANES) // members
     each = devices * cap
-    diagonal = iota((each, each), 0) == iota((each, each), 1)
+    halves = members // CAP
     lane = iota((each, LANES), 1)
-    weights = turned(got_ref[:, :, members * width :].reshape(each, LANES).astype(F32))
-    scores = jnp.zeros((each, LANES), F32)
-    copies = []
-    grams, inverses = {}, {}
-
-    def take(member):
-        rows_s[member] = got_ref[:, :, member * width : (member + 1) * width].reshape(each, width)
-
-
-    def norms(member):
-        for start in range(0, each, CHUNK):
-            wider = rows_s[member, start : start + CHUNK, :].astype(F32)
-            square_sum = jnp.sum(wider * wider, axis=1, keepdims=True)
-            unit = wider * lax.rsqrt(square_sum + 1e-06)
-            unit_s[member, start : start + CHUNK, :] = unit.astype(BF16)
-
-    def products(member):
-        grams[member] = dot(unit_s[member], unit_s[member], ((1,), (1,)))
-
-    def weigh(member, scores):
-        gram = grams[member]
-        sharp = sharp_ref[member : member + 1, :]
-        rate = sharp * LOG2_E
-        cosine = jnp.where(diagonal, F32(0.0), gram)
-        expo = weights[member : member + 1, :] * jnp.exp2(rate * cosine - rate)
-        total = jnp.sum(expo, axis=1, keepdims=True)
-        prob_s[member] = expo.astype(BF16)
-        inverses[member] = 1.0 / total
-        return jnp.where(lane == member, jnp.log(total) + sharp[:, 0:LANES], scores)
-
-    def smooth(member, index):
-        of = slice(index * BLOCK, (index + 1) * BLOCK)
-        numer = dot(prob_s[member], rows_s[member, :, of])
-        done_s[member, :, of] = (numer * inverses[member]).astype(BF16)
-
-    def give(member, last):
-        first = member * width
-        back_s[:, :, first : first + width] = done_s[member].reshape(devices, cap, width)
-        copies.append(
-            pltpu.make_async_copy(
-                back_s.at[:, :, first:last], back_hbm.at[:, :, first:last], sems.at[member]
+    tile = got_ref[:, :, members * width :].reshape(each, LANES).astype(F32)
+    crowd = jnp.where(lane == members, tile, F32(0.0))
+    most = jnp.max(jnp.max(crowd, axis=1, keepdims=True), axis=0, keepdims=True)
+    most_ref[...] = jnp.broadcast_to(most, most_ref.shape).astype(jnp.int32)
+    crowded = jnp.max(most) > CAP
+
+    def way(is_short):
+        odd = iota((each, 1), 0) % CAP == 1
+        diagonal = iota((each, each), 0) == iota((each, each), 1)
+        weights = turned(tile)
+        scores = jnp.zeros((each, LANES), F32)
+        grams, inverses, chosen, copies = {}, {}, [], []
+
+        def first_rows(value):
+            return jnp.where(odd, pltpu.roll(value, 1, 0), value)
+
+        def second_rows(value):
+            return jnp.where(odd, value, pltpu.roll(value, each - 1, 0))
+
+        if is_short:
+            held = (second_rows(tile) > 0).astype(F32)
+            before = jnp.zeros((each, 1), F32)
+            for member in range(members):
+                mine = held[:, member : member + 1]
+                chosen.append((mine > 0) & (before == odd.astype(F32)))
+                before = before + mine
+
+        def take(member):
+            rows_s[member * each : (member + 1) * each, :] = got_ref[
+                :, :, member * width : (member + 1) * width
+            ].reshape(each, width)
+            for start in range(member * each, (member + 1) * each, CHUNK):
+                wider = rows_s[start : start + CHUNK, :].astype(F32)
+                square_sum = jnp.sum(wider * wider, axis=1, keepdims=True)
+                unit = wider * lax.rsqrt(square_sum + 1e-06)
+                unit_s[start : start + CHUNK, :] = unit.astype(BF16)
+
+        def products(member):
+            unit = unit_s[member * each : (member + 1) * each, :]
+            grams[member] = dot(unit, unit, ((1,), (1,)))
+
+        def weigh(member, scores):
+            sharp = sharp_ref[member : member + 1, :]
+            rate = sharp * LOG2_E
+            cosine = jnp.where(diagonal, F32(0.0), grams[member])
+            expo = weights[member : member + 1, :] * jnp.exp2(rate * cosine - rate)
+            total = jnp.sum(expo, axis=1, keepdims=True)
+            inverses[member] = 1.0 / total
+            if is_short:
+                half, at = member // CAP, member % CAP * each
+                here = odd if member % CAP == 1 else ~odd
+                left = jnp.where(here, first_rows(expo), F32(0.0))
+                left_s[half, :, at : at + each] = left.astype(BF16)
+                left = jnp.where(chosen[member], second_rows(expo), F32(0.0))
+                left_s[halves + half, :, at : at + each] = left.astype(BF16)
+            else:
+                prob_s[member] = expo.astype(BF16)
+            return jnp.where(lane == member, jnp.log(total) + sharp[:, 0:LANES], scores)
+
+        def share(index, scores, is_last):
+            if not is_short:
+                left, inverse = prob_s[index], inverses[index]
+                low, high = index * each, (index + 1) * each
+            elif index < halves:
+                own = range(index * CAP, (index + 1) * CAP)
+                left = left_s[index]
+                inverse = jnp.where(odd, first_rows(inverses[own[1]]), inverses[own[0]])
+                low, high = own[0] * each, (own[-1] + 1) * each
+            else:
+                left = jnp.concatenate([left_s[halves + half] for half in range(halves)], axis=1)
+                inverse = jnp.zeros((each, 1), F32)
+                for member in range(members):
+                    inverse = jnp.where(chosen[member], second_rows(inverses[member]), inverse)
+                low, high = 0, members * each
+            for start in range(0, width, BLOCK):
+                of = slice(start, start + BLOCK)
+                done_s[index, :, of] = (dot(left, rows_s[low:high, of]) * inverse).astype(BF16)
+            first, last = index * width, (index + 1) * width
+            sent_s[:, :, first:last] = done_s[index].reshape(devices, cap, width)
+            if is_last:
+                sent_s[:, :, last : last + LANES] = scores.astype(BF16).reshape(devices, cap, LANES)
+                last = last + LANES
+            to = short_hbm if is_short else full_hbm
+            copies.append(
+                pltpu.make_async_copy(
+                    sent_s.at[:, :, first:last], to.at[:, :, first:last], sems.at[index]
+                )
             )
-        )
-        copies[-1].start()
-
-    pairs = [tuple(range(at, min(at + 2, members))) for at in range(0, members, 2)]
-    for member in pairs[0]:
-        take(member)
-        norms(member)
-    for turn in range(len(pairs) + 2):
-        if turn < len(pairs):
-            for member in pairs[turn]:
+            copies[-1].start()
+
+        for half in range(halves):
+            own = range(half * CAP, (half + 1) * CAP)
+            for member in own:
+                take(member)
+            for member in own:
                 products(member)
-        if turn + 1 < len(pairs):
-            for member in pairs[turn + 1]:
-                take(member)
-                norms(member)
-        if turn < len(pairs):
-            for member in pairs[turn]:
+            for member in own:
                 scores = weigh(member, scores)
-        if turn == len(pairs) - 1:
-            back_s[:, :, members * width :] = scores.astype(BF16).reshape(devices, cap, LANES)
-        if 1 <= turn <= len(pairs):
-            for member in pairs[turn - 1]:
-                for index in range(width // BLOCK):
-                    smooth(member, index)
-                give(member, wide if member == members - 1 else (member + 1) * width)
-    for copy in copies:
-        copy.wait()
+            if half > 0:
+                for index in range((half - 1) * CAP, half * CAP):
+                    share(index // CAP if is_short else index, scores, False)
+                    if is_short:
+                        break
+        if is_short:
+            share(halves - 1, scores, False)
+            share(halves, scores, True)
+        else:
+            for index in range((halves - 1) * CAP, members):
+                share(index, scores, index == members - 1)
+        for copy in copies:
+            copy.wait()
+
+    @pl.when(jnp.logical_not(crowded))
+    def _():
+        way(True)
+
+    @pl.when(crowded)
+    def _():
+        way(False)
 
 
 def clusters(sharp, got):
     members = sharp.shape[0]
     devices, cap, wide = got.shape
     width = (wide - LANES) // members
+    each = devices * cap
+    blocks = members // CAP + 1
+    short = (devices, cap, blocks * width + LANES)
     return pl.pallas_call(
         cluster_kernel,
-        out_shape=pltpu.HBM(got.shape, BF16),
+        out_shape=(
+            pltpu.HBM(short, BF16),
+            pltpu.HBM(got.shape, BF16),
+            jax.ShapeDtypeStruct((1, LANES), jnp.int32),
+        ),
         in_specs=[IN_VMEM] * 2,
-        out_specs=IN_HBM,
+        out_specs=(IN_HBM, IN_HBM, IN_VMEM),
         scratch_shapes=[
-            pltpu.VMEM((members, devices * cap, width), BF16),
-            pltpu.VMEM((members, devices * cap, width), BF16),
-            pltpu.VMEM((members, devices * cap, devices * cap), BF16),
-            pltpu.VMEM((members, devices * cap, width), BF16),
+            pltpu.VMEM((members * each, width), BF16),
+            pltpu.VMEM((members * each, width), BF16),
+            pltpu.VMEM((members, each, each), BF16),
+            pltpu.VMEM((2 * (members // CAP), each, CAP * each), BF16),
+            pltpu.VMEM((members, each, width), BF16),
             pltpu.VMEM(got.shape, BF16),
             pltpu.SemaphoreType.DMA((members,)),
         ],
-        compiler_params=pltpu.CompilerParams(vmem_limit_bytes=20 * MIB),
+        compiler_params=pltpu.CompilerParams(vmem_limit_bytes=24 * MIB),
         name="clusters",
     )(sharp, got)
 
 
-def home_kernel(members, hot_ref, place_ref, home_ref, smooth_hbm, score_hbm, rows_s, smooth_s, score_s, sems):
+def home_kernel(hot_ref, place_ref, home_ref, smooth_hbm, score_hbm, rows_s, smooth_s, score_s, sems):
     count, width = smooth_s.shape
     devices, cap, wide = home_ref.shape
-    blocks = 2
+    blocks = HALVES
+    members = (wide - LANES) // width
     each = devices * cap
     scores = home_ref[:, :, members * width :].reshape(each, LANES)
     taken = turned(dot(hot_ref[:, members * each :], scores))
@@ -298,15 +384,11 @@
         copy.wait()
 
 
-def bring_home(hot, place, home, members):
+def bring_home(hot, place, home, width):
     count = hot.shape[0]
-    width = (home.shape[2] - LANES) // members
-
-    def kernel(*refs):
-        home_kernel(members, *refs)
-
+    members = (home.shape[2] - LANES) // width
     return pl.pallas_call(
-        kernel,
+        home_kernel,
         out_shape=(jax.ShapeDtypeStruct((count, width), BF16), jax.ShapeDtypeStruct((count,), BF16)),
         in_specs=[IN_VMEM] * 3,
         out_specs=(IN_HBM, IN_HBM),
@@ -330,10 +412,14 @@
     )
     got = lax.all_to_all(send, "own", split_axis=0, concat_axis=0, tiled=True)
     sharp = jnp.broadcast_to(group_sharpness.astype(F32)[:, None], (members, devices * CAP))
-    back = clusters(sharp, got)
-    hot = hot_rows(place, devices, members)
-    home = lax.all_to_all(back, "own", split_axis=0, concat_axis=0, tiled=True)
-    return bring_home(hot, place, home, members)
+    short, full, most = clusters(sharp, got)
+    hot_full, hot_short = hot_rows(place, devices, members)
+
+    def back(sent, hot):
+        home = lax.all_to_all(sent, "own", split_axis=0, concat_axis=0, tiled=True)
+        return tuple(bring_home(hot, place, home, sentence_vectors.shape[1]))
+
+    return lax.cond(most[0, 0] > CAP, lambda: back(full, hot_full), lambda: back(short, hot_short))
 
 
 def solution(mesh):

time: 88.4 us -> 83.7 us (0.947)
  blocking collectives: 42.3 us -> 30.2 us
  starting transfers between devices: 4.74 us -> 11.5 us
  Pallas kernels: 9.68 us -> 11.7 us
  waiting for transfers between devices: 30.6 us -> 29.2 us
    all_to_all x1, blocking collectives: 42.3 us -> 30.2 us  [back(): home = lax.all_to_all(sent, 'own', split_axis=0, concat_axis=0, tiled=True)]
    all_to_all x1, starting transfers between devices: 4.74 us -> 11.5 us  [local(): got = lax.all_to_all(send, 'own', split_axis=0, concat_axis=0, tiled=True)]
    pallas_call x3, Pallas kernels: 6.08 us -> 8 us  [the longest x1 4.42 us: clusters(): pl.pallas_call(cluster_kernel, out_shape=(pltpu.HBM(short, BF16), pltpu.H...]
    all_to_all x1, waiting for transfers between devices: 30.6 us -> 29.2 us  [local(): got = lax.all_to_all(send, 'own', split_axis=0, concat_axis=0, tiled=True)]
  transfers between devices with their start and end apart: 1 -> 1, of which waited for: 1 -> 1; matrix products, arithmetic and copies ran while one was open for 0% -> 0% of each run, Pallas kernels for 0% -> 2%
where the time goes in v4:
time: 83.7 us; the launch traced here: 83.4 us
  blocking collectives  30.2 us (36%)
  waiting for transfers between devices  29.2 us (35%)
  Pallas kernels  11.7 us (14%)
  starting transfers between devices  11.5 us (14%)
    all_to_all x1, blocking collectives, back(): home = lax.all_to_all(sent, 'own', split_axis=0, concat_axis=0, tiled=True)  30.2 us
    all_to_all x1, waiting for transfers between devices, local(): got = lax.all_to_all(send, 'own', split_axis=0, concat_axis=0, tiled=True)  29.2 us
    all_to_all x1, starting transfers between devices, local(): got = lax.all_to_all(send, 'own', split_axis=0, concat_axis=0, tiled=True)  11.5 us
    pallas_call x1, Pallas kernels, clusters(): pl.pallas_call(cluster_kernel, out_shape=(pltpu.HBM(short, BF16), pltpu.H...  4.42 us
    pallas_call x1, Pallas kernels, pack(): pl.pallas_call(kernel, out_shape=(pltpu.HBM((devices, CAP, wide), BF16),...  3.68 us
    pallas_call x1, Pallas kernels, bring_home(): pl.pallas_call(home_kernel, out_shape=(jax.ShapeDtypeStruct((count, width...  1.94 us
  transfers between devices with their start and end apart: 1, of which 1 were waited for; matrix products, arithmetic and copies ran while one was open for 0% of the time, Pallas kernels for 2%

profile of v4, /device:TPU:1, one launch (start us, length us, event | category | flops | bytes accessed | tf_op | source)
XLA Modules:
  0.0 83.4 jit_solution(4992519421988768847)
XLA Ops:
  0.6 3.7 %pack.1 = (bf16[128,2,4224]{2,1,0:T(2,128)(2,1)}, s32[3,512]{1,0:T(4,128)}) custom-call(s32[1,512]{1,0:T(1,128)} %bitcast.4, bf16[512]{0:T(512)(128)(2,1)} %refs_1_.1, bf16[512,1024]{1,0:T(8,128)(2,1)} %refs_2_.1), custom_call_target="tpu_custom_call" | custom-call | flops 1073741824 | bytes 4194304 | tf_op jit(solution)/shard_map/pack/pallas_call | solution.py:134
  4.3 0.0 copy-start.1
  4.3 0.0 copy-start.2
  4.3 11.5 %all-to-all-start.2 = ((bf16[128,2,4224]{2,1,0:T(2,128)(2,1)}), bf16[128,2,4224]{2,1,0:T(2,128)(2,1)S(1)}, u32[]{:S(2)}, u32[]{:S(2)}) async-start(bf16[128,2,4224]{2,1,0:T(2,128)(2,1)} %get-tuple-element.27), calls=%async_computation.2 | async-start | bytes 4325376 | tf_op jit(solution)/shard_map/all_to_all | solution.py:413
  15.8 0.0 copy-done.1
  15.8 1.6 %hot_rows.1 = (bf16[512,1280]{1,0:T(8,128)(2,1)S(1)}, bf16[512,1024]{1,0:T(8,128)(2,1)}) custom-call(s32[3,512]{1,0:T(4,128)S(1)} %copy-done.1), custom_call_target="tpu_custom_call" | custom-call | flops 1048576 | bytes 2097152 | tf_op jit(solution)/shard_map/hot_rows/pallas_call | solution.py:189
  17.5 29.2 %all-to-all-done.2.got_ref = bf16[128,2,4224]{2,1,0:T(2,128)(2,1)S(1)} async-done(((bf16[128,2,4224]{2,1,0:T(2,128)(2,1)}), bf16[128,2,4224]{2,1,0:T(2,128)(2,1)S(1)}, u32[]{:S(2)}, u32[]{:S(2)}) %all-to-all-start.2) | async-done | bytes 2162720 | tf_op jit(solution)/shard_map/all_to_all | solution.py:413
  46.6 0.0 copy-done.2
  46.7 0.0 copy-start
  46.7 0.1 broadcast_in_dim.2.sharp_ref
  46.7 4.4 %clusters.1 = (bf16[128,2,3200]{2,1,0:T(2,128)(2,1)}, bf16[128,2,4224]{2,1,0:T(2,128)(2,1)}, s32[1,128]{1,0:T(1,128)S(1)}) custom-call(f32[4,256]{1,0:T(4,128)S(1)} %broadcast_in_dim.2.sharp_ref, bf16[128,2,4224]{2,1,0:T(2,128)(2,1)S(1)} %all-to-all-done.2.got_ref), custom_call_target="tpu_custom_call" | custom-call | tf_op jit(solution)/shard_map/clusters/pallas_call | solution.py:339
  51.2 0.0 copy-done
  51.2 32.1 %conditional.1 = ((bf16[512,1024]{1,0:T(8,128)(2,1)}, bf16[512]{0:T(512)(128)(2,1)})) conditional(s32[]{:T(128)} %bitcast.1, (bf16[128,2,3200]{2,1,0:T(2,128)(2,1)}, bf16[512,1024]{1,0:T(8,128)(2,1)S(1)}, s32[3,512]{1,0:T(4,128)S(1)}) %tuple.24, (bf16[128,2,4224]{2,1,0:T(2,128)(2,1)}, bf16[512,1280]{1,0:T(8,128)(2,1)S(1)}, ...), branch_computations={%region_0.0_spmd, %region_1.0_spmd} | conditional | bytes 4325384 | solution.py:422
  51.2 30.2 %all_to_all.13.home_ref = bf16[128,2,3200]{2,1,0:T(2,128)(2,1)S(1)} all-to-all(bf16[128,2,3200]{2,1,0:T(2,128)(2,1)} %get-tuple-element.14), channel_id=1, replica_groups=mesh['own'=128] {'own'}, dimensions={0} | all-to-all | bytes 3276800 | tf_op jit(solution)/shard_map/cond/branch_0_fun/all_to_all | solution.py:419
  81.4 1.9 %bring_home.2 = (bf16[512,1024]{1,0:T(8,128)(2,1)}, bf16[512]{0:T(512)(128)(2,1)}) custom-call(bf16[512,1024]{1,0:T(8,128)(2,1)S(1)} %get-tuple-element.12.hot_ref, s32[3,512]{1,0:T(4,128)S(1)} %get-tuple-element.13.place_ref, bf16[128,2,3200]{2,1,0:T(2,128)(2,1)S(1)} %all_to_all.13.home_ref), custom_call_target="tpu_custom_call" | custom-call | tf_op jit(solution)/shard_map/cond/branch_0_fun/bring_home/pallas_call | solution.py:390
Async XLA Ops:
  4.3 11.5 %copy-start.1 = (s32[3,512]{1,0:T(4,128)S(1)}, s32[3,512]{1,0:T(4,128)}, u32[]{:S(2)}) copy-start(s32[3,512]{1,0:T(4,128)} %get-tuple-element.30.refs_0_) | copy-start | bytes 18436
  4.3 42.3 %copy-start.2 = (bf16[4]{0:T(256)(128)(2,1)S(1)}, bf16[4]{0:T(256)(128)(2,1)}, u32[]{:S(2)}) copy-start(bf16[4]{0:T(256)(128)(2,1)} %param.9) | copy-start | bytes 28
  4.3 42.3 %all-to-all-start.2 = ((bf16[128,2,4224]{2,1,0:T(2,128)(2,1)}), bf16[128,2,4224]{2,1,0:T(2,128)(2,1)S(1)}, u32[]{:S(2)}, u32[]{:S(2)}) async-start(bf16[128,2,4224]{2,1,0:T(2,128)(2,1)} %get-tuple-element.27), calls=%async_computation.2 | async-start | bytes 4325376 | tf_op jit(solution)/shard_map/all_to_all | solution.py:413
  46.7 4.5 %copy-start = (bf16[512,1024]{1,0:T(8,128)(2,1)S(1)}, bf16[512,1024]{1,0:T(8,128)(2,1)}, u32[]{:S(2)}) copy-start(bf16[512,1024]{1,0:T(8,128)(2,1)} %get-tuple-element.31) | copy-start | bytes 3145732

commit v5 on v4

--- a/solution.py
+++ b/solution.py
@@ -221,11 +221,12 @@
         scores = jnp.zeros((each, LANES), F32)
         grams, inverses, chosen, copies = {}, {}, [], []
 
-        def first_rows(value):
-            return jnp.where(odd, pltpu.roll(value, 1, 0), value)
+        def turn(value, shift):
+            split = value.reshape(each // 8, 8, value.shape[1])
+            return pltpu.roll(split, shift, 1).reshape(value.shape)
 
         def second_rows(value):
-            return jnp.where(odd, value, pltpu.roll(value, each - 1, 0))
+            return jnp.where(odd, value, turn(value, 7))
 
         if is_short:
             held = (second_rows(tile) > 0).astype(F32)
@@ -258,8 +259,10 @@
             inverses[member] = 1.0 / total
             if is_short:
                 half, at = member // CAP, member % CAP * each
-                here = odd if member % CAP == 1 else ~odd
-                left = jnp.where(here, first_rows(expo), F32(0.0))
+                if member % CAP == 1:
+                    left = jnp.where(odd, turn(expo, 1), F32(0.0))
+                else:
+                    left = jnp.where(odd, F32(0.0), expo)
                 left_s[half, :, at : at + each] = left.astype(BF16)
                 left = jnp.where(chosen[member], second_rows(expo), F32(0.0))
                 left_s[halves + half, :, at : at + each] = left.astype(BF16)
@@ -274,7 +277,7 @@
             elif index < halves:
                 own = range(index * CAP, (index + 1) * CAP)
                 left = left_s[index]
-                inverse = jnp.where(odd, first_rows(inverses[own[1]]), inverses[own[0]])
+                inverse = jnp.where(odd, turn(inverses[own[1]], 1), inverses[own[0]])
                 low, high = own[0] * each, (own[-1] + 1) * each
             else:
                 left = jnp.concatenate([left_s[halves + half] for half in range(halves)], axis=1)
@@ -302,7 +305,6 @@
             own = range(half * CAP, (half + 1) * CAP)
             for member in own:
                 take(member)
-            for member in own:
                 products(member)
             for member in own:
                 scores = weigh(member, scores)

time: 83.7 us -> 88.9 us (1.062)
  blocking collectives: 30.2 us -> 35.9 us
    all_to_all x1, blocking collectives: 30.2 us -> 35.9 us  [back(): home = lax.all_to_all(sent, 'own', split_axis=0, concat_axis=0, tiled=True)]
where the time goes in v5:
time: 88.9 us; the launch traced here: 88.6 us
  blocking collectives  35.9 us (40%)
  waiting for transfers between devices  29.2 us (33%)
  starting transfers between devices  11.5 us (13%)
  Pallas kernels  11.2 us (13%)
    all_to_all x1, blocking collectives, back(): home = lax.all_to_all(sent, 'own', split_axis=0, concat_axis=0, tiled=True)  35.9 us
    all_to_all x1, waiting for transfers between devices, local(): got = lax.all_to_all(send, 'own', split_axis=0, concat_axis=0, tiled=True)  29.2 us
    all_to_all x1, starting transfers between devices, local(): got = lax.all_to_all(send, 'own', split_axis=0, concat_axis=0, tiled=True)  11.5 us
    pallas_call x1, Pallas kernels, clusters(): pl.pallas_call(cluster_kernel, out_shape=(pltpu.HBM(short, BF16), pltpu.H...  3.7 us
    pallas_call x1, Pallas kernels, pack(): pl.pallas_call(kernel, out_shape=(pltpu.HBM((devices, CAP, wide), BF16),...  3.68 us
    pallas_call x1, Pallas kernels, bring_home(): pl.pallas_call(home_kernel, out_shape=(jax.ShapeDtypeStruct((count, width...  2.16 us
  transfers between devices with their start and end apart: 1, of which 1 were waited for; matrix products, arithmetic and copies ran while one was open for 0% of the time, Pallas kernels for 2%

profile of v5, /device:TPU:1, one launch (start us, length us, event | category | flops | bytes accessed | tf_op | source)
XLA Modules:
  0.0 88.6 jit_solution(15936111685893013911)
XLA Ops:
  0.6 3.7 %pack.1 = (bf16[128,2,4224]{2,1,0:T(2,128)(2,1)}, s32[3,512]{1,0:T(4,128)}) custom-call(s32[1,512]{1,0:T(1,128)} %bitcast.4, bf16[512]{0:T(512)(128)(2,1)} %refs_1_.1, bf16[512,1024]{1,0:T(8,128)(2,1)} %refs_2_.1), custom_call_target="tpu_custom_call" | custom-call | flops 1073741824 | bytes 4194304 | tf_op jit(solution)/shard_map/pack/pallas_call | solution.py:134
  4.3 0.0 copy-start.1
  4.3 0.0 copy-start.2
  4.3 11.5 %all-to-all-start.2 = ((bf16[128,2,4224]{2,1,0:T(2,128)(2,1)}), bf16[128,2,4224]{2,1,0:T(2,128)(2,1)S(1)}, u32[]{:S(2)}, u32[]{:S(2)}) async-start(bf16[128,2,4224]{2,1,0:T(2,128)(2,1)} %get-tuple-element.27), calls=%async_computation.2 | async-start | bytes 4325376 | tf_op jit(solution)/shard_map/all_to_all | solution.py:415
  15.8 0.0 copy-done.1
  15.8 1.6 %hot_rows.1 = (bf16[512,1280]{1,0:T(8,128)(2,1)S(1)}, bf16[512,1024]{1,0:T(8,128)(2,1)}) custom-call(s32[3,512]{1,0:T(4,128)S(1)} %copy-done.1), custom_call_target="tpu_custom_call" | custom-call | flops 1048576 | bytes 2097152 | tf_op jit(solution)/shard_map/hot_rows/pallas_call | solution.py:189
  17.5 29.2 %all-to-all-done.2.got_ref = bf16[128,2,4224]{2,1,0:T(2,128)(2,1)S(1)} async-done(((bf16[128,2,4224]{2,1,0:T(2,128)(2,1)}), bf16[128,2,4224]{2,1,0:T(2,128)(2,1)S(1)}, u32[]{:S(2)}, u32[]{:S(2)}) %all-to-all-start.2) | async-done | bytes 2162720 | tf_op jit(solution)/shard_map/all_to_all | solution.py:415
  46.6 0.0 copy-done.2
  46.7 0.0 copy-start
  46.7 0.1 broadcast_in_dim.2.sharp_ref
  46.7 3.7 %clusters.1 = (bf16[128,2,3200]{2,1,0:T(2,128)(2,1)}, bf16[128,2,4224]{2,1,0:T(2,128)(2,1)}, s32[1,128]{1,0:T(1,128)S(1)}) custom-call(f32[4,256]{1,0:T(4,128)S(1)} %broadcast_in_dim.2.sharp_ref, bf16[128,2,4224]{2,1,0:T(2,128)(2,1)S(1)} %all-to-all-done.2.got_ref), custom_call_target="tpu_custom_call" | custom-call | tf_op jit(solution)/shard_map/clusters/pallas_call | solution.py:341
  50.5 0.0 copy-done
  50.5 38.1 %conditional.1 = ((bf16[512,1024]{1,0:T(8,128)(2,1)}, bf16[512]{0:T(512)(128)(2,1)})) conditional(s32[]{:T(128)} %bitcast.1, (bf16[128,2,3200]{2,1,0:T(2,128)(2,1)}, bf16[512,1024]{1,0:T(8,128)(2,1)S(1)}, s32[3,512]{1,0:T(4,128)S(1)}) %tuple.24, (bf16[128,2,4224]{2,1,0:T(2,128)(2,1)}, bf16[512,1280]{1,0:T(8,128)(2,1)S(1)}, ...), branch_computations={%region_0.0_spmd, %region_1.0_spmd} | conditional | bytes 4325384 | solution.py:424
  50.5 35.9 %all_to_all.14.home_ref = bf16[128,2,4224]{2,1,0:T(2,128)(2,1)S(1)} all-to-all(bf16[128,2,4224]{2,1,0:T(2,128)(2,1)} %get-tuple-element.17), channel_id=1, replica_groups=mesh['own'=128] {'own'}, dimensions={0} | all-to-all | bytes 4325376 | tf_op jit(solution)/shard_map/cond/branch_1_fun/all_to_all | solution.py:421
  86.4 2.2 %bring_home.3 = (bf16[512,1024]{1,0:T(8,128)(2,1)}, bf16[512]{0:T(512)(128)(2,1)}) custom-call(bf16[512,1280]{1,0:T(8,128)(2,1)S(1)} %get-tuple-element.15.hot_ref, s32[3,512]{1,0:T(4,128)S(1)} %get-tuple-element.16.place_ref, bf16[128,2,4224]{2,1,0:T(2,128)(2,1)S(1)} %all_to_all.14.home_ref), custom_call_target="tpu_custom_call" | custom-call | tf_op jit(solution)/shard_map/cond/branch_1_fun/bring_home/pallas_call | solution.py:392
Async XLA Ops:
  4.3 11.5 %copy-start.1 = (s32[3,512]{1,0:T(4,128)S(1)}, s32[3,512]{1,0:T(4,128)}, u32[]{:S(2)}) copy-start(s32[3,512]{1,0:T(4,128)} %get-tuple-element.30.refs_0_) | copy-start | bytes 18436
  4.3 42.3 %copy-start.2 = (bf16[4]{0:T(256)(128)(2,1)S(1)}, bf16[4]{0:T(256)(128)(2,1)}, u32[]{:S(2)}) copy-start(bf16[4]{0:T(256)(128)(2,1)} %param.9) | copy-start | bytes 28
  4.3 42.3 %all-to-all-start.2 = ((bf16[128,2,4224]{2,1,0:T(2,128)(2,1)}), bf16[128,2,4224]{2,1,0:T(2,128)(2,1)S(1)}, u32[]{:S(2)}, u32[]{:S(2)}) async-start(bf16[128,2,4224]{2,1,0:T(2,128)(2,1)} %get-tuple-element.27), calls=%async_computation.2 | async-start | bytes 4325376 | tf_op jit(solution)/shard_map/all_to_all | solution.py:415
  46.7 3.8 %copy-start = (bf16[512,1024]{1,0:T(8,128)(2,1)S(1)}, bf16[512,1024]{1,0:T(8,128)(2,1)}, u32[]{:S(2)}) copy-start(bf16[512,1024]{1,0:T(8,128)(2,1)} %get-tuple-element.31) | copy-start | bytes 3145732
